TPU v7x, 32 devices: a whole 2x2x4 slice. The times are simulated.
32 devices in a mesh: groups: 2 (over x), tm: 16 (over z, y, core).
Axes of the slice: x: 2, y: 2, z: 4, core: 2. Of those that a mesh axis runs over, the one named last changes fastest.
Arguments:
- features: bfloat16 [32768, 80], P(('groups', 'tm')), parts along dimension 0, may hold values from -6 to 6
- stem_kernel: bfloat16 [3, 3, 256], replicated, may hold values from -3 to 3
- mid_depthwise: bfloat16 [3, 3, 256], replicated, may hold values from -3 to 3
- mid_pointwise: bfloat16 [256, 256], replicated, may hold values from -0.5 to 0.5
- last_depthwise: bfloat16 [3, 3, 256], replicated, may hold values from -3 to 3
- last_pointwise: bfloat16 [256, 256], replicated, may hold values from -0.5 to 0.5
- proj_weight: bfloat16 [2560, 1024], replicated, may hold values from -0.15625 to 0.15625
- norm_gain: float32 [1024], replicated, may hold values from 0.25 to 1.75
- qkv_weight: bfloat16 [1024, 3072], replicated
- out_weight: bfloat16 [1024, 1024], replicated, may hold values from -0.1875 to 0.1875
- cotangent: bfloat16 [4096, 1024], P(('groups', 'tm')), parts along dimension 0, may hold values from -6 to 6
- utt_bounds: int32 [16, 2], P('groups'), parts along dimension 0, may hold values from 0 to 2048, as said below
- live_blocks: int32 [32, 7], P(('groups', 'tm')), parts along dimension 0, may hold values from 0 to 1, as said below
Outputs:
- block_out: bfloat16 [4096, 1024], P(('groups', 'tm')), parts along dimension 0
- frame_grads: bfloat16 [4096, 1024], P(('groups', 'tm')), parts along dimension 0
- proj_grads: float32 [5120, 1024], P(('groups', 'tm')), parts along dimension 0
There are 2 independent parts, one for each index of `groups`. A program takes and returns all parts, laid end to end along the dimension named above; an argument that names none is the same for every part. Nothing has to cross between parts.
Inputs may be any that keep to these rules, and one draw needn't show every extreme that they name: `utt_bounds`: rows are in order of time and tile frames 0 to 2048 without gaps; each utterance has 1 to 384 frames and one has exactly 384. `live_blocks`: entry [b, c] is 1 iff some utterance has frames in block b (frames b * 128 to (b + 1) * 128 - 1) and in block b + c - 3; it is 0 where that block lies outside the recording.
All inputs are finite; a program needn't handle non-finite values.
Results may differ from a plain program's by a relative error of at most 0.015.
Values may be sent and summed in bfloat16 or wider, within the bound.
A program may use at most 128 MiB of HBM per device.

v0:
```python
import jax
import jax.numpy as jnp
from jax import lax
from jax.sharding import PartitionSpec as P

HEADS = 8
REACH = 3
HEAD_DIM = 128


norm_eps = 1e-05
neg_fill = -1e30


def passed_along(x, axis, by):
    size = lax.axis_size(axis)
    pairs = [(i, i + by) for i in range(size) if 0 <= i + by < size]
    return lax.ppermute(x, axis, pairs)


def shortened(x):
    return jax.tree.map(lambda a: a.astype(jnp.bfloat16) if a.dtype == jnp.float32 else a, x)


def conv_valid(inputs, kernel, groups):
    result = lax.conv_general_dilated(
        inputs[None],
        kernel,
        (2, 2),
        ((0, 0), (1, 1)),
        dimension_numbers=("NHWC", "HWIO", "NHWC"),
        feature_group_count=groups,
        preferred_element_type=jnp.float32,
    )
    return result[0]


def pointwise(depth_out, weight):
    in_shape = depth_out.shape
    mixed_rows = jnp.dot(
        depth_out.reshape(-1, in_shape[-1]), weight, preferred_element_type=jnp.float32
    )
    return jax.nn.relu(mixed_rows).reshape(in_shape[:-1] + (weight.shape[1],)).astype(jnp.bfloat16)


def with_rim(local_rows):
    rim_rows = passed_along(local_rows[-1:], "tm", 1)
    return jnp.concatenate([rim_rows, local_rows], axis=0)


def subsample(features, stem_kernel, mid_depthwise, mid_pointwise, last_depthwise, last_pointwise):
    channels = stem_kernel.shape[-1]
    stem_taps = stem_kernel[:, :, None, :]
    mid_taps = mid_depthwise[:, :, None, :]
    last_taps = last_depthwise[:, :, None, :]
    first_section = jax.nn.relu(conv_valid(with_rim(features)[:, :, None], stem_taps, 1)).astype(
        jnp.bfloat16
    )
    mid_depth = conv_valid(with_rim(first_section), mid_taps, channels).astype(jnp.bfloat16)
    second_section = pointwise(mid_depth, mid_pointwise)
    last_depth = conv_valid(with_rim(second_section), last_taps, channels).astype(jnp.bfloat16)
    return pointwise(last_depth, last_pointwise)


def segment_of(positions, utt_bounds):
    inside = (utt_bounds[None, :, 0] <= positions[:, None]) & (
        positions[:, None] < utt_bounds[None, :, 1]
    )
    number = jnp.arange(utt_bounds.shape[0], dtype=jnp.int32)
    found = jnp.sum(jnp.where(inside, number[None, :], 0), axis=1)
    return jnp.where(jnp.any(inside, axis=1), found, -1)


def masked_scores(query_part, key_part, allowed):
    scores = jnp.einsum(
        "qhd,khd->hqk", query_part, key_part, preferred_element_type=jnp.float32
    ) * HEAD_DIM ** (-0.5)
    return jnp.where(allowed[None], scores, neg_fill)


def score_grads(query_part, key_part, value_part, dout_part, log_norm, delta_part, allowed):
    scores = masked_scores(query_part, key_part, allowed)
    weights_full = jnp.exp(scores - log_norm[..., None])
    dprob = jnp.einsum("qhd,khd->hqk", dout_part, value_part, preferred_element_type=jnp.float32)
    dscore = (weights_full * (dprob - delta_part[..., None])).astype(jnp.bfloat16)
    return (weights_full.astype(jnp.bfloat16), dscore)


def per_device(
    features,
    stem_kernel,
    mid_depthwise,
    mid_pointwise,
    last_depthwise,
    last_pointwise,
    proj_weight,
    norm_gain,
    qkv_weight,
    out_weight,
    cotangent,
    utt_bounds,
    live_blocks,
):
    frame_rows = cotangent.shape[0]
    model_width = cotangent.shape[1]
    window_rows = (2 * REACH + 1) * frame_rows
    head_group = min(4, HEADS)
    score_scale = HEAD_DIM ** (-0.5)
    third_section = subsample(
        features, stem_kernel, mid_depthwise, mid_pointwise, last_depthwise, last_pointwise
    )
    flat_rows = third_section.reshape(frame_rows, -1)
    frames = jnp.dot(flat_rows, proj_weight, preferred_element_type=jnp.float32).astype(
        jnp.bfloat16
    )
    frames_f = frames.astype(jnp.float32)
    row_mean = jnp.mean(frames_f, axis=-1, keepdims=True)
    centered = frames_f - row_mean
    inv_std = lax.rsqrt(jnp.mean(centered * centered, axis=-1, keepdims=True) + norm_eps)
    normalized = centered * inv_std
    normed = (normalized * norm_gain).astype(jnp.bfloat16)
    projected = jnp.dot(normed, qkv_weight, preferred_element_type=jnp.float32).astype(jnp.bfloat16)
    query_local = projected[:, :model_width]
    keys_local = projected[:, model_width : 2 * model_width]
    values_local = projected[:, 2 * model_width :]
    my_index = lax.axis_index("tm")
    local_seg = segment_of(
        my_index * frame_rows + jnp.arange(frame_rows, dtype=jnp.int32), utt_bounds
    )
    window_seg = segment_of(
        my_index * frame_rows - REACH * frame_rows + jnp.arange(window_rows, dtype=jnp.int32),
        utt_bounds,
    )
    block_flag = jnp.repeat(live_blocks[0], frame_rows, total_repeat_length=window_rows)
    key_mask = (local_seg[:, None] == window_seg[None, :]) & (block_flag[None, :] == 1)
    key_value = jnp.stack([keys_local, values_local])
    lower_blocks = []
    moving = key_value
    for offset in range(REACH):
        moving = passed_along(moving, "tm", 1)
        lower_blocks.append(moving)
    upper_blocks = []
    moving = key_value
    for offset in range(REACH):
        moving = passed_along(moving, "tm", -1)
        upper_blocks.append(moving)
    window_pairs = jnp.concatenate(lower_blocks[::-1] + [key_value] + upper_blocks, axis=1)
    window_keys = window_pairs[0].reshape(window_rows, HEADS, HEAD_DIM)
    window_values = window_pairs[1].reshape(window_rows, HEADS, HEAD_DIM)
    query_heads = query_local.reshape(frame_rows, HEADS, HEAD_DIM)
    out_parts = []
    norm_parts = []
    for first_head in range(0, HEADS, head_group):
        picked = slice(first_head, first_head + head_group)
        scores = masked_scores(query_heads[:, picked], window_keys[:, picked], key_mask)
        row_max = jnp.max(scores, axis=-1)
        log_norm = row_max + jnp.log(jnp.sum(jnp.exp(scores - row_max[..., None]), axis=-1))
        probs = jnp.exp(scores - log_norm[..., None]).astype(jnp.bfloat16)
        out_parts.append(
            jnp.einsum(
                "hqk,khd->qhd", probs, window_values[:, picked], preferred_element_type=jnp.float32
            ).astype(jnp.bfloat16)
        )
        norm_parts.append(log_norm)
    attention = jnp.concatenate(out_parts, axis=1).reshape(frame_rows, model_width)
    log_norms = jnp.concatenate(norm_parts, axis=0)
    block_out = (
        frames_f + jnp.dot(attention, out_weight, preferred_element_type=jnp.float32)
    ).astype(jnp.bfloat16)
    d_attention = lax.dot_general(
        cotangent, out_weight, (((1,), (1,)), ((), ())), preferred_element_type=jnp.float32
    ).astype(jnp.bfloat16)
    d_heads = d_attention.reshape(frame_rows, HEADS, HEAD_DIM)
    delta = jnp.sum(
        (d_attention.astype(jnp.float32) * attention.astype(jnp.float32)).reshape(
            frame_rows, HEADS, HEAD_DIM
        ),
        axis=-1,
    ).T
    query_grads = []
    key_parts = []
    value_parts = []
    for first_head in range(0, HEADS, head_group):
        picked = slice(first_head, first_head + head_group)
        probs_low, dscore = score_grads(
            query_heads[:, picked],
            window_keys[:, picked],
            window_values[:, picked],
            d_heads[:, picked],
            log_norms[picked],
            delta[picked],
            key_mask,
        )
        query_grads.append(
            score_scale
            * jnp.einsum(
                "hqk,khd->qhd", dscore, window_keys[:, picked], preferred_element_type=jnp.float32
            )
        )
        key_parts.append(
            score_scale
            * jnp.einsum(
                "hqk,qhd->khd", dscore, query_heads[:, picked], preferred_element_type=jnp.float32
            )
        )
        value_parts.append(
            jnp.einsum(
                "hqk,qhd->khd", probs_low, d_heads[:, picked], preferred_element_type=jnp.float32
            )
        )
    grad_query = (
        jnp.concatenate(query_grads, axis=1).reshape(frame_rows, model_width).astype(jnp.bfloat16)
    )
    partials = jnp.stack(
        [
            jnp.concatenate(key_parts, axis=1).reshape(window_rows, model_width),
            jnp.concatenate(value_parts, axis=1).reshape(window_rows, model_width),
        ]
    )

    def piece_at(offset):
        return lax.slice_in_dim(
            partials, (offset + REACH) * frame_rows, (offset + REACH + 1) * frame_rows, axis=1
        )

    downward = jnp.zeros((2, frame_rows, model_width), jnp.float32)
    for offset in range(REACH, 0, -1):
        downward = passed_along(shortened(downward + piece_at(-offset)), "tm", -1)
    upward = jnp.zeros((2, frame_rows, model_width), jnp.float32)
    for offset in range(REACH, 0, -1):
        upward = passed_along(shortened(upward + piece_at(offset)), "tm", 1)
    key_grads = downward + upward + piece_at(0)
    grad_key = key_grads[0].astype(jnp.bfloat16)
    grad_value = key_grads[1].astype(jnp.bfloat16)
    grad_normed = lax.dot_general(
        jnp.concatenate([grad_query, grad_key, grad_value], axis=1),
        qkv_weight,
        (((1,), (1,)), ((), ())),
        preferred_element_type=jnp.float32,
    )
    scaled_grad = grad_normed * norm_gain
    ln_grad = inv_std * (
        scaled_grad
        - jnp.mean(scaled_grad, axis=-1, keepdims=True)
        - normalized * jnp.mean(scaled_grad * normalized, axis=-1, keepdims=True)
    )
    frame_grads = (cotangent.astype(jnp.float32) + ln_grad).astype(jnp.bfloat16)
    flat_cols = lax.slice_in_dim(
        flat_rows, 0, lax.axis_size("tm") * (flat_rows.shape[1] // lax.axis_size("tm")), axis=1
    )
    proj_grads = lax.psum_scatter(
        lax.dot_general(
            flat_cols, frame_grads, (((0,), (0,)), ((), ())), preferred_element_type=jnp.float32
        ).astype(jnp.bfloat16),
        "tm",
        scatter_dimension=0,
        tiled=True,
    ).astype(jnp.float32)
    return (block_out, frame_grads, proj_grads)


def solution(mesh):
    in_specs = (
        P(("groups", "tm"), None),
        P(),
        P(),
        P(),
        P(),
        P(),
        P(),
        P(),
        P(),
        P(),
        P(("groups", "tm"), None),
        P("groups", None),
        P(("groups", "tm"), None),
    )
    out_specs = (P(("groups", "tm"), None), P(("groups", "tm"), None), P(("groups", "tm"), None))
    return jax.shard_map(
        per_device, mesh=mesh, in_specs=in_specs, out_specs=out_specs, check_vma=False
    )
```

profile of v0, /device:TPU:0, one launch (start us, length us, event | category | flops | bytes accessed | tf_op | source)
XLA Modules:
  0.0 383.0 jit_solution(3781969373001177030)
XLA Ops:
  7.2 0.9 slice.127
  8.2 2.3 collective-permute-start
  11.3 1.6 fusion.105
  13.0 4.5 %fusion.90 = s32[896]{0:T(1024)S(1)} fusion(s32[1,1,7,128]{3,2,1,0:T(8,128)S(1)} %get-tuple-element.53, s32[1,1,7,128]{3,2,1,0:T(8,128)S(1)} %get-tuple-element.52, s32[]{:T(128)} %bitcast.23, s32[]{:T(128)} %bitcast.24, s32[]{:T(128)} %bitcast.25, s32[]{:T(128)} %bitcast.26, s32[]{:T(128)} %bitcast.27, s32[]{:T(128)} %bitcast.29, s32[]{:T(128)} %bitcast.28), kind=kLoop, calls=%fused_computation.167 | loop fusion | flops 12544 | bytes 10780 | tf_op jit(solution)/shard_map/jit(_take)/gather | solution.py:134
  17.5 1.0 maximum_bitcast_fusion.2
  18.8 11.2 %copy.107 = bf16[1025,8,14,1]{1,3,2,0:T(2,128)(2,1)} copy(bf16[1025,8,14,1]{0,2,1,3:T(8,128)(2,1)S(1)} %fusion.63) | data formatting | bytes 459200 | tf_op jit(solution)/shard_map/conv_general_dilated | solution.py:26
  30.0 15.4 %maximum_convert_fusion = bf16[512,8,6,256]{3,1,2,0:T(8,128)(2,1)S(1)} fusion(pred[8,6]{0,1:T(8,128)(4,1)S(1)} %copy-done.33, bf16[1025,8,14,1]{1,3,2,0:T(2,128)(2,1)} %copy.107, bf16[3,3,1,256]{3,1,0,2:T(4,128)(2,1)S(1)} %bitcast.180), kind=kOutput, calls=%fused_computation.2 | convolution fusion | flops 132120576 | bytes 12817168 | tf_op jit(solution)/shard_map/conv_general_dilated | solution.py:26
  45.4 9.3 %copy.110 = bf16[512,8,6,256]{3,0,2,1:T(8,128)(2,1)} copy(bf16[512,8,6,256]{3,1,2,0:T(8,128)(2,1)S(1)} %maximum_convert_fusion) | data formatting | bytes 25165824 | tf_op jit(solution)/shard_map/convert_element_type | solution.py:56
  54.8 5.1 %collective-permute-start.1 = (bf16[1,40,256]{2,1,0:T(8,128)(2,1)S(1)}, bf16[1,40,256]{2,1,0:T(8,128)(2,1)S(1)}, u32[]{:S(2)}, u32[]{:S(2)}) collective-permute-start(bf16[1,40,256]{2,1,0:T(8,128)(2,1)S(1)} %slice_bitcast_fusion.7), channel_id=1, source_target_pairs={{0,1},{1,2},{2,3},{3,4},{4,5},{5,6},{6,7},{7,8},{8,9},{9,10},{10,1... | collective-permute-start | bytes 61448 | tf_op jit(solution)/shard_map/ppermute | solution.py:18
  59.9 9.0 %slice_bitcast_fusion = bf16[512,40,256]{2,0,1:T(8,128)(2,1)} fusion(bf16[512,1,48,256]{3,0,2,1:T(8,128)(2,1)} %bitcast.165), kind=kLoop, calls=%fused_computation.23 | loop fusion | bytes 20971520 | tf_op jit(solution)/shard_map/convert_element_type | solution.py:56
  69.0 6.4 %maximum_bitcast_fusion = bf16[513,1,40,256]{3,0,2,1:T(8,128)(2,1)S(1)} fusion(bf16[512,40,256]{2,0,1:T(8,128)(2,1)} %slice_bitcast_fusion, bf16[1,40,256]{2,0,1:T(2,128)(2,1)S(1)} %copy.111), kind=kLoop, calls=%fused_computation.22 | loop fusion | flops 21012480 | bytes 21012480 | tf_op jit(solution)/shard_map/broadcast_in_dim | solution.py:27
  75.4 2.3 pad.5
  77.8 27.3 %copy.113 = bf16[513,1,8,6,256]{4,2,3,0,1:T(8,128)(2,1)S(1)} copy(bf16[513,1,8,6,256]{4,0,3,2,1:T(8,128)(2,1)S(1)} %bitcast.164) | data formatting | bytes 25214976 | tf_op jit(solution)/shard_map/conv_general_dilated | solution.py:26
  105.0 1.0 slice.186
  106.1 5.3 %select_convert_fusion = bf16[256,8,3,256]{3,1,2,0:T(8,128)(2,1)S(1)} fusion(pred[8,3]{0,1:T(4,128)(4,1)S(1)} %copy-done.35, bf16[513,1,7,2,256]{4,2,3,0,1:T(8,128)(2,1)S(1)} %slice.186, bf16[513,1,8,6,256]{4,2,3,0,1:T(8,128)(2,1)S(1)} %copy.113, bf16[3,3,1,256]{3,1,0,2:T(4,128)(2,1)S(1)} %bitcast.181), kind=kOutput, calls=%fused_computation.34 | convolution fusion | flops 81887232 | bytes 19435032 | tf_op jit(solution)/shard_map/conv_general_dilated | solution.py:26
  112.4 3.2 copy.116
  115.5 5.2 %convert_element_type.139 = bf16[5120,256]{1,0:T(8,128)(2,1)} reshape(bf16[256,1,20,256]{3,2,0,1:T(8,128)(2,1)} %copy.116) | data formatting | bytes 5242880 | tf_op jit(solution)/shard_map/convert_element_type | solution.py:59
  120.7 2.6 fusion.11
  123.3 1.5 copy-done.7
  124.8 2.1 collective-permute-start.2
  127.0 5.1 %convert_element_type.141 = bf16[256,20,256]{2,1,0:T(8,128)(2,1)} reshape(bf16[5120,256]{1,0:T(8,128)(2,1)} %copy-done.7) | data formatting | bytes 5242880 | tf_op jit(solution)/shard_map/convert_element_type | solution.py:43
  132.1 2.2 maximum_bitcast_fusion.1
  135.2 2.4 copy.119
  138.3 1.9 select_convert_fusion.1
  141.0 1.1 convert_element_type.143
  142.1 2.3 fusion.20
  144.3 1.9 convert_element_type.145
  146.2 3.4 fusion.106
  149.9 3.9 %convolution_convert_fusion.1 = bf16[128,3072]{1,0:T(8,128)(2,1)S(1)} fusion(bf16[1024,3072]{1,0:T(8,128)(2,1)} %param.23, f32[128,1024]{1,0:T(8,128)S(1)} %get-tuple-element.46, f32[1024]{0:T(1024)S(1)} %copy-done.26, f32[128]{0:T(128)S(1)} %add_rsqrt_fusion, f32[128]{0:T(128)S(1)} %broadcast_multiply_fusion.2), kind=kOutput, calls=%fused_computation.38 | convolution fusion | flops 806223872 | bytes 7607296 | tf_op jit(solution)/shard_map/dot_general | solution.py:122
  153.9 3.5 collective-permute-start.3
  157.6 1.3 collective-permute-start.6
  159.0 12.1 %collective-permute-start.4 = (bf16[2,128,1024]{2,1,0:T(8,128)(2,1)S(1)}, bf16[2,128,1024]{2,1,0:T(8,128)(2,1)S(1)}, u32[]{:S(2)}, u32[]{:S(2)}) collective-permute-start(bf16[2,128,1024]{2,1,0:T(8,128)(2,1)S(1)} %collective-permute-done.3), channel_id=1, source_target_pairs={{0,1},{1,2},{2,3},{3,4},{4,5},{5,6},{6,7},{7,8},{8,9},{9,10},{10,1... | collective-permute-start | bytes 1572872 | tf_op jit(solution)/shard_map/ppermute | solution.py:18
  171.3 0.8 convolution_convert_fusion.3
  172.1 1.3 collective-permute-start.7
  173.4 13.8 %collective-permute-start.5 = (bf16[2,128,1024]{2,1,0:T(8,128)(2,1)S(1)}, bf16[2,128,1024]{2,1,0:T(8,128)(2,1)S(1)}, u32[]{:S(2)}, u32[]{:S(2)}) collective-permute-start(bf16[2,128,1024]{2,1,0:T(8,128)(2,1)S(1)} %collective-permute-done.4), channel_id=1, source_target_pairs={{0,1},{1,2},{2,3},{3,4},{4,5},{5,6},{6,7},{7,8},{8,9},{9,10},{10,1... | collective-permute-start | bytes 1572872 | tf_op jit(solution)/shard_map/ppermute | solution.py:18
  187.2 0.8 compare_and_fusion
  188.1 0.8 fusion.102
  189.1 1.5 collective-permute-start.8
  190.9 4.0 %collective-permute-done.8 = bf16[2,128,1024]{2,1,0:T(8,128)(2,1)S(1)} collective-permute-done((bf16[2,128,1024]{2,1,0:T(8,128)(2,1)S(1)}, bf16[2,128,1024]{2,1,0:T(8,128)(2,1)S(1)}, u32[]{:S(2)}, u32[]{:S(2)}) %collective-permute-start.8) | collective-permute-done | bytes 524320 | tf_op jit(solution)/shard_map/ppermute | solution.py:18
  194.9 2.0 slice_bitcast_fusion.1
  197.4 1.8 fusion.101
  199.2 3.8 copy.152
  203.1 1.9 fusion.108
  208.4 0.9 copy.131
  209.2 1.1 multiply_bitcast_fusion.2
  210.3 0.9 copy.165
  211.2 1.9 reduce_sum.87
  213.1 1.6 fusion.104
  214.7 0.9 copy.132
  215.6 0.9 copy.136
  216.6 2.2 convolution_bitcast_fusion
  223.1 9.1 %collective-permute-start.12 = (bf16[2,128,1024]{1,2,0:T(8,128)(2,1)S(1)}, bf16[2,128,1024]{1,2,0:T(8,128)(2,1)S(1)}, u32[]{:S(2)}, u32[]{:S(2)}) collective-permute-start(bf16[2,128,1024]{1,2,0:T(8,128)(2,1)S(1)} %get-tuple-element.19), channel_id=1, source_target_pairs={{0,1},{1,2},{2,3},{3,4},{4,5},{5,6},{6,7},{7,8},{8,9},{9,10},{10,1... | collective-permute-start | bytes 1572872 | tf_op jit(solution)/shard_map/ppermute | solution.py:18
  232.2 1.3 collective-permute-start.9
  233.8 14.3 %collective-permute-start.13 = (bf16[2,128,1024]{1,2,0:T(8,128)(2,1)S(1)}, bf16[2,128,1024]{1,2,0:T(8,128)(2,1)S(1)}, u32[]{:S(2)}, u32[]{:S(2)}) collective-permute-start(bf16[2,128,1024]{1,2,0:T(8,128)(2,1)S(1)} %fusion.43), channel_id=1, source_target_pairs={{0,1},{1,2},{2,3},{3,4},{4,5},{5,6},{6,7},{7,8},{8,9},{9,10},{10,1... | collective-permute-start | bytes 1572872 | tf_op jit(solution)/shard_map/ppermute | solution.py:18
  248.1 1.5 collective-permute-done.13
  249.8 1.3 collective-permute-start.10
  251.1 15.4 %collective-permute-start.14 = (bf16[2,128,1024]{1,2,0:T(8,128)(2,1)S(1)}, bf16[2,128,1024]{1,2,0:T(8,128)(2,1)S(1)}, u32[]{:S(2)}, u32[]{:S(2)}) collective-permute-start(bf16[2,128,1024]{1,2,0:T(8,128)(2,1)S(1)} %get-tuple-element.17), channel_id=1, source_target_pairs={{0,1},{1,2},{2,3},{3,4},{4,5},{5,6},{6,7},{7,8},{8,9},{9,10},{10,1... | collective-permute-start | bytes 1572872 | tf_op jit(solution)/shard_map/ppermute | solution.py:18
  266.6 1.5 collective-permute-start.11
  269.3 7.8 %collective-permute-done.11 = bf16[2,128,1024]{1,2,0:T(8,128)(2,1)S(1)} collective-permute-done((bf16[2,128,1024]{1,2,0:T(8,128)(2,1)S(1)}, bf16[2,128,1024]{1,2,0:T(8,128)(2,1)S(1)}, u32[]{:S(2)}, u32[]{:S(2)}) %collective-permute-start.11) | collective-permute-done | bytes 524320 | tf_op jit(solution)/shard_map/ppermute | solution.py:18
  277.4 2.4 fusion.99
  280.8 3.9 %convolution_convert_fusion = bf16[2560,1024]{1,0:T(8,128)(2,1)} fusion(bf16[128,2560]{1,0:T(8,128)(2,1)S(1)} %convert_element_type.145, bf16[128,1024]{1,0:T(8,128)(2,1)S(1)} %add_convert_fusion), kind=kOutput, calls=%fused_computation.35 | convolution fusion | flops 673710080 | bytes 6160384 | tf_op jit(solution)/shard_map/dot_general | solution.py:252
  284.7 1.2 fusion.28
  285.9 88.2 %reduce-scatter.2.cloned.1.call-done = bf16[160,1024]{1,0:T(8,128)(2,1)} async-done(((bf16[2560,1024]{1,0:T(8,128)(2,1)}), bf16[160,1024]{1,0:T(8,128)(2,1)}) %reduce-scatter.2.cloned.1.call-update) | async-done | bytes 327696 | tf_op jit(solution)/shard_map/reduce_scatter | solution.py:251
  374.1 1.9 convert_element_type.177
  (163 shorter events, 16.5 us)
Async XLA Ops:
  7.2 164.1 %copy-start = (bf16[1024,1024]{1,0:T(8,128)(2,1)S(1)}, bf16[1024,1024]{1,0:T(8,128)(2,1)}, u32[]{:S(2)}) copy-start(bf16[1024,1024]{1,0:T(8,128)(2,1)} %param.24) | copy-start | bytes 6291460
  7.2 366.9 %reduce-scatter.2.cloned.1.call-start = ((), (), s32[]{:S(2)}) async-start(), calls=%async_computation.1 | async-start | bytes 5570560 | tf_op jit(solution)/shard_map/reduce_scatter | solution.py:251
  8.2 9.3 %collective-permute-start = (bf16[1,80]{0,1:T(8,128)(2,1)S(1)}, bf16[1,80]{0,1:T(8,128)(2,1)S(1)}, u32[]{:S(2)}, u32[]{:S(2)}) collective-permute-start(bf16[1,80]{0,1:T(8,128)(2,1)S(1)} %slice.127), channel_id=1, source_target_pairs={{0,1},{1,2},{2,3},{3,4},{4,5},{5,6},{6,7},{7,8},{8,9},{9,10},{10,1... | collective-permute-start | bytes 488 | tf_op jit(solution)/shard_map/ppermute | solution.py:18
  18.7 11.2 %copy-start.30 = (bf16[3,3,256]{2,1,0:T(4,128)(2,1)S(1)}, bf16[3,3,256]{2,1,0:T(4,128)(2,1)}, u32[]{:S(2)}) copy-start(bf16[3,3,256]{2,1,0:T(4,128)(2,1)} %param.16) | copy-start | bytes 13828
  18.8 11.2 %copy-start.33 = (pred[8,6]{0,1:T(8,128)(4,1)S(1)}, pred[8,6]{0,1:T(8,128)(4,1)}, u32[]{:S(2)}) copy-start(pred[8,6]{0,1:T(8,128)(4,1)} %constant.135) | copy-start | bytes 148
  54.8 14.1 %collective-permute-start.1 = (bf16[1,40,256]{2,1,0:T(8,128)(2,1)S(1)}, bf16[1,40,256]{2,1,0:T(8,128)(2,1)S(1)}, u32[]{:S(2)}, u32[]{:S(2)}) collective-permute-start(bf16[1,40,256]{2,1,0:T(8,128)(2,1)S(1)} %slice_bitcast_fusion.7), channel_id=1, source_target_pairs={{0,1},{1,2},{2,3},{3,4},{4,5},{5,6},{6,7},{7,8},{8,9},{9,10},{10,1... | collective-permute-start | bytes 61448 | tf_op jit(solution)/shard_map/ppermute | solution.py:18
  105.0 1.1 copy-start.31
  105.0 1.1 copy-start.35
  115.5 5.2 %copy-start.21 = (bf16[256,256]{1,0:T(8,128)(2,1)S(1)}, bf16[256,256]{1,0:T(8,128)(2,1)}, u32[]{:S(2)}) copy-start(bf16[256,256]{1,0:T(8,128)(2,1)} %param.18) | copy-start | bytes 393220
  123.3 1.5 copy-start.7
  124.8 7.3 %collective-permute-start.2 = (bf16[1,20,256]{2,1,0:T(8,128)(2,1)S(1)}, bf16[1,20,256]{2,1,0:T(8,128)(2,1)S(1)}, u32[]{:S(2)}, u32[]{:S(2)}) collective-permute-start(bf16[1,20,256]{2,1,0:T(8,128)(2,1)S(1)} %slice_bitcast_fusion.8), channel_id=1, source_target_pairs={{0,1},{1,2},{2,3},{3,4},{4,5},{5,6},{6,7},{7,8},{8,9},{9,10},{10,1... | collective-permute-start | bytes 30728 | tf_op jit(solution)/shard_map/ppermute | solution.py:18
  137.6 0.7 copy-start.32
  137.6 0.7 copy-start.34
  140.2 1.9 copy-start.22
  146.2 3.7 copy-start.26
  149.7 4.2 %copy-start.24 = (f32[128]{0:T(128)}, f32[128]{0:T(128)S(1)}, u32[]{:S(2)}) copy-start(f32[128]{0:T(128)S(1)} %broadcast_multiply_fusion.2) | copy-start | bytes 1540
  149.9 3.9 %copy-start.28 = (f32[128]{0:T(128)}, f32[128]{0:T(128)S(1)}, u32[]{:S(2)}) copy-start(f32[128]{0:T(128)S(1)} %add_rsqrt_fusion) | copy-start | bytes 1540
  149.9 21.4 %copy-start.11 = (bf16[128,1024]{1,0:T(8,128)(2,1)S(1)}, bf16[128,1024]{1,0:T(8,128)(2,1)}, u32[]{:S(2)}) copy-start(bf16[128,1024]{1,0:T(8,128)(2,1)} %param.25) | copy-start | bytes 786436
  153.9 5.0 %collective-permute-start.3 = (bf16[2,128,1024]{2,1,0:T(8,128)(2,1)S(1)}, bf16[2,128,1024]{2,1,0:T(8,128)(2,1)S(1)}, u32[]{:S(2)}, u32[]{:S(2)}) collective-permute-start(bf16[2,128,1024]{2,1,0:T(8,128)(2,1)S(1)} %pad_maximum_fusion.3), channel_id=1, source_target_pairs={{0,1},{1,2},{2,3},{3,4},{4,5},{5,6},{6,7},{7,8},{8,9},{9,10},{10,1... | collective-permute-start | bytes 1572872 | tf_op jit(solution)/shard_map/ppermute | solution.py:18
  157.6 14.5 %collective-permute-start.6 = (bf16[2,128,1024]{2,1,0:T(8,128)(2,1)S(1)}, bf16[2,128,1024]{2,1,0:T(8,128)(2,1)S(1)}, u32[]{:S(2)}, u32[]{:S(2)}) collective-permute-start(bf16[2,128,1024]{2,1,0:T(8,128)(2,1)S(1)} %pad_maximum_fusion.3), channel_id=1, source_target_pairs={{1,0},{2,1},{3,2},{4,3},{5,4},{6,5},{7,6},{8,7},{9,8},{10,9},{11,1... | collective-permute-start | bytes 1572872 | tf_op jit(solution)/shard_map/ppermute | solution.py:18
  159.0 14.4 %collective-permute-start.4 = (bf16[2,128,1024]{2,1,0:T(8,128)(2,1)S(1)}, bf16[2,128,1024]{2,1,0:T(8,128)(2,1)S(1)}, u32[]{:S(2)}, u32[]{:S(2)}) collective-permute-start(bf16[2,128,1024]{2,1,0:T(8,128)(2,1)S(1)} %collective-permute-done.3), channel_id=1, source_target_pairs={{0,1},{1,2},{2,3},{3,4},{4,5},{5,6},{6,7},{7,8},{8,9},{9,10},{10,1... | collective-permute-start | bytes 1572872 | tf_op jit(solution)/shard_map/ppermute | solution.py:18
  172.1 18.7 %copy-start.8 = (bf16[128,1024]{1,0:T(8,128)(2,1)}, bf16[128,1024]{1,0:T(8,128)(2,1)S(1)}, u32[]{:S(2)}) copy-start(bf16[128,1024]{1,0:T(8,128)(2,1)S(1)} %convolution_convert_fusion.3) | copy-start | bytes 786436
  172.1 16.9 %collective-permute-start.7 = (bf16[2,128,1024]{2,1,0:T(8,128)(2,1)S(1)}, bf16[2,128,1024]{2,1,0:T(8,128)(2,1)S(1)}, u32[]{:S(2)}, u32[]{:S(2)}) collective-permute-start(bf16[2,128,1024]{2,1,0:T(8,128)(2,1)S(1)} %collective-permute-done.6), channel_id=1, source_target_pairs={{1,0},{2,1},{3,2},{4,3},{5,4},{6,5},{7,6},{8,7},{9,8},{10,9},{11,1... | collective-permute-start | bytes 1572872 | tf_op jit(solution)/shard_map/ppermute | solution.py:18
  173.4 17.1 %collective-permute-start.5 = (bf16[2,128,1024]{2,1,0:T(8,128)(2,1)S(1)}, bf16[2,128,1024]{2,1,0:T(8,128)(2,1)S(1)}, u32[]{:S(2)}, u32[]{:S(2)}) collective-permute-start(bf16[2,128,1024]{2,1,0:T(8,128)(2,1)S(1)} %collective-permute-done.4), channel_id=1, source_target_pairs={{0,1},{1,2},{2,3},{3,4},{4,5},{5,6},{6,7},{7,8},{8,9},{9,10},{10,1... | collective-permute-start | bytes 1572872 | tf_op jit(solution)/shard_map/ppermute | solution.py:18
  189.0 14.0 %copy-start.17 = (bf16[128,4,128]{2,1,0:T(4,128)(2,1)}, bf16[128,4,128]{2,1,0:T(4,128)(2,1)S(1)}, u32[]{:S(2)}) copy-start(bf16[128,4,128]{2,1,0:T(4,128)(2,1)S(1)} %get-tuple-element.32) | copy-start | bytes 393220
  189.0 16.4 %copy-start.19 = (bf16[128,4,128]{2,1,0:T(4,128)(2,1)}, bf16[128,4,128]{2,1,0:T(4,128)(2,1)S(1)}, u32[]{:S(2)}) copy-start(bf16[128,4,128]{2,1,0:T(4,128)(2,1)S(1)} %get-tuple-element.33) | copy-start | bytes 393220
  189.1 5.8 %collective-permute-start.8 = (bf16[2,128,1024]{2,1,0:T(8,128)(2,1)S(1)}, bf16[2,128,1024]{2,1,0:T(8,128)(2,1)S(1)}, u32[]{:S(2)}, u32[]{:S(2)}) collective-permute-start(bf16[2,128,1024]{2,1,0:T(8,128)(2,1)S(1)} %collective-permute-done.7), channel_id=1, source_target_pairs={{1,0},{2,1},{3,2},{4,3},{5,4},{6,5},{7,6},{8,7},{9,8},{10,9},{11,1... | collective-permute-start | bytes 1572872 | tf_op jit(solution)/shard_map/ppermute | solution.py:18
  203.1 2.4 copy-start.14
  203.1 2.4 copy-start.23
  205.0 2.8 copy-start.3
  205.0 2.2 copy-start.1
  206.1 1.6 copy-start.5
  216.6 2.3 copy-start.2
  216.6 2.7 copy-start.6
  216.6 2.7 copy-start.10
  216.6 3.3 copy-start.4
  216.6 3.3 copy-start.9
  219.8 1.1 copy-start.20
  220.4 1.0 copy-start.18
  223.1 10.6 %collective-permute-start.12 = (bf16[2,128,1024]{1,2,0:T(8,128)(2,1)S(1)}, bf16[2,128,1024]{1,2,0:T(8,128)(2,1)S(1)}, u32[]{:S(2)}, u32[]{:S(2)}) collective-permute-start(bf16[2,128,1024]{1,2,0:T(8,128)(2,1)S(1)} %get-tuple-element.19), channel_id=1, source_target_pairs={{0,1},{1,2},{2,3},{3,4},{4,5},{5,6},{6,7},{7,8},{8,9},{9,10},{10,1... | collective-permute-start | bytes 1572872 | tf_op jit(solution)/shard_map/ppermute | solution.py:18
  232.2 15.9 %collective-permute-start.9 = (bf16[2,128,1024]{1,2,0:T(8,128)(2,1)S(1)}, bf16[2,128,1024]{1,2,0:T(8,128)(2,1)S(1)}, u32[]{:S(2)}, u32[]{:S(2)}) collective-permute-start(bf16[2,128,1024]{1,2,0:T(8,128)(2,1)S(1)} %get-tuple-element.20), channel_id=1, source_target_pairs={{1,0},{2,1},{3,2},{4,3},{5,4},{6,5},{7,6},{8,7},{9,8},{10,9},{11,1... | collective-permute-start | bytes 1572872 | tf_op jit(solution)/shard_map/ppermute | solution.py:18
  233.8 15.8 %collective-permute-start.13 = (bf16[2,128,1024]{1,2,0:T(8,128)(2,1)S(1)}, bf16[2,128,1024]{1,2,0:T(8,128)(2,1)S(1)}, u32[]{:S(2)}, u32[]{:S(2)}) collective-permute-start(bf16[2,128,1024]{1,2,0:T(8,128)(2,1)S(1)} %fusion.43), channel_id=1, source_target_pairs={{0,1},{1,2},{2,3},{3,4},{4,5},{5,6},{6,7},{7,8},{8,9},{9,10},{10,1... | collective-permute-start | bytes 1572872 | tf_op jit(solution)/shard_map/ppermute | solution.py:18
  249.8 16.7 %collective-permute-start.10 = (bf16[2,128,1024]{1,2,0:T(8,128)(2,1)S(1)}, bf16[2,128,1024]{1,2,0:T(8,128)(2,1)S(1)}, u32[]{:S(2)}, u32[]{:S(2)}) collective-permute-start(bf16[2,128,1024]{1,2,0:T(8,128)(2,1)S(1)} %get-tuple-element.18), channel_id=1, source_target_pairs={{1,0},{2,1},{3,2},{4,3},{5,4},{6,5},{7,6},{8,7},{9,8},{10,9},{11,1... | collective-permute-start | bytes 1572872 | tf_op jit(solution)/shard_map/ppermute | solution.py:18
  251.1 17.1 %copy-start.16 = (bf16[896,4,128]{2,1,0:T(4,128)(2,1)S(1)}, bf16[896,4,128]{2,1,0:T(4,128)(2,1)}, u32[]{:S(2)}) copy-start(bf16[896,4,128]{2,1,0:T(4,128)(2,1)} %get-tuple-element.23) | copy-start | bytes 2752516
  251.1 17.6 %copy-start.15 = (bf16[896,4,128]{2,1,0:T(4,128)(2,1)S(1)}, bf16[896,4,128]{2,1,0:T(4,128)(2,1)}, u32[]{:S(2)}) copy-start(bf16[896,4,128]{2,1,0:T(4,128)(2,1)} %get-tuple-element.24) | copy-start | bytes 2752516
  251.1 18.2 %collective-permute-start.14 = (bf16[2,128,1024]{1,2,0:T(8,128)(2,1)S(1)}, bf16[2,128,1024]{1,2,0:T(8,128)(2,1)S(1)}, u32[]{:S(2)}, u32[]{:S(2)}) collective-permute-start(bf16[2,128,1024]{1,2,0:T(8,128)(2,1)S(1)} %get-tuple-element.17), channel_id=1, source_target_pairs={{0,1},{1,2},{2,3},{3,4},{4,5},{5,6},{6,7},{7,8},{8,9},{9,10},{10,1... | collective-permute-start | bytes 1572872 | tf_op jit(solution)/shard_map/ppermute | solution.py:18
  266.6 10.5 %collective-permute-start.11 = (bf16[2,128,1024]{1,2,0:T(8,128)(2,1)S(1)}, bf16[2,128,1024]{1,2,0:T(8,128)(2,1)S(1)}, u32[]{:S(2)}, u32[]{:S(2)}) collective-permute-start(bf16[2,128,1024]{1,2,0:T(8,128)(2,1)S(1)} %fusion.40), channel_id=1, source_target_pairs={{1,0},{2,1},{3,2},{4,3},{5,4},{6,5},{7,6},{8,7},{9,8},{10,9},{11,1... | collective-permute-start | bytes 1572872 | tf_op jit(solution)/shard_map/ppermute | solution.py:18
  268.7 8.6 %slice-start = ((s8[6291456]{0:T(1024)(128)(4,1)}), s8[4194304]{0:T(1024)(128)(4,1)S(1)}, s32[]{:S(2)}) async-start(s8[6291456]{0:T(1024)(128)(4,1)} %bitcast.169), calls=%async_computation.2 | async-start | bytes 8388608
  269.3 8.1 %slice-start.1 = ((s8[6291456]{0:T(1024)(128)(4,1)}), s8[2097152]{0:T(1024)(128)(4,1)S(1)}, s32[]{:S(2)}) async-start(s8[6291456]{0:T(1024)(128)(4,1)} %bitcast.169), calls=%async_computation.3 | async-start | bytes 4194304
  269.3 8.1 %copy-start.25 = (f32[128]{0:T(128)S(1)}, f32[128]{0:T(128)}, u32[]{:S(2)}) copy-start(f32[128]{0:T(128)} %copy-done.24) | copy-start | bytes 1540
  269.3 8.1 %copy-start.27 = (f32[1024]{0:T(1024)S(1)}, f32[1024]{0:T(1024)}, u32[]{:S(2)}) copy-start(f32[1024]{0:T(1024)} %param.22) | copy-start | bytes 12292
  269.3 8.1 %copy-start.29 = (f32[128]{0:T(128)S(1)}, f32[128]{0:T(128)}, u32[]{:S(2)}) copy-start(f32[128]{0:T(128)} %copy-done.28) | copy-start | bytes 1540
  277.4 2.4 copy-start.12
  280.1 0.7 copy-start.13
Sparse Core Ops, SparseCore 0:
  284.8 89.1 reduce-scatter.1
where the time goes:
time: 389 us; the launch traced here: 383 us
  local copies, waits for them, and re-layouts  104 us (27%)
  waiting for transfers between devices  102 us (26%)
  starting transfers between devices  86 us (22%)
  matrix products  52.3 us (13%)
  other arithmetic  23.5 us (6%)
  between operations  15.5 us (4%)
    reduce_scatter x1, waiting for transfers between devices, per_device(): lax.psum_scatter(lax.dot_general(flat_cols, frame_grads, (((0,), (0,)), (...  88.2 us
    ppermute x15, starting transfers between devices, passed_along(): return lax.ppermute(x, axis, pairs)  86 us
    conv_general_dilated x7, local copies, waits for them, and re-layouts, conv_valid(): lax.conv_general_dilated(inputs[None], kernel, (2, 2), ((0, 0), (1, 1)),...  42.6 us
    conv_general_dilated x3, matrix products, conv_valid(): lax.conv_general_dilated(inputs[None], kernel, (2, 2), ((0, 0), (1, 1)),...  22.5 us
    convert_element_type x5, local copies, waits for them, and re-layouts, subsample(): jax.nn.relu(conv_valid(with_rim(features)[:, :, None], stem_taps, 1))  18.4 us
    ppermute x15, waiting for transfers between devices, passed_along(): return lax.ppermute(x, axis, pairs)  13.5 us
    convert_element_type x4, local copies, waits for them, and re-layouts, subsample(): conv_valid(with_rim(first_section), mid_taps, channels).astype(jnp.bfloat16)  9.35 us
    broadcast_in_dim x2, other arithmetic, conv_valid(): inputs[None]  8.66 us
  transfers between devices with their start and end apart: 16, of which 6 were waited for; matrix products, arithmetic and copies ran while one was open for 7% of the time, Pallas kernels for 0%

commit v1 on v0

v1 whole, which is shorter than its diff:
```python
import functools

import jax
import jax.numpy as jnp
from jax import lax
from jax.experimental import pallas as pl
from jax.experimental.pallas import tpu as pltpu
from jax.sharding import PartitionSpec as P

HEADS = 8
REACH = 3
HEAD_DIM = 128
norm_eps = 1e-05
neg_fill = -1e30
MEL_PITCH = 84
SCALE = HEAD_DIM ** (-0.5)


def dot_nt(a, b):
    return lax.dot_general(a, b, (((1,), (1,)), ((), ())), preferred_element_type=jnp.float32)


def dot_tn(a, b):
    return lax.dot_general(a, b, (((0,), (0,)), ((), ())), preferred_element_type=jnp.float32)


def dot_nn(a, b):
    return jnp.dot(a, b, preferred_element_type=jnp.float32)


def subsample_kernel(
    x_ref, stem_ref, mid_dw_ref, mid_pw_ref, last_dw_ref, last_pw_ref, flat_ref, even, odd, second, shifted
):
    rows = x_ref.shape[0] // 4
    main = rows - 8
    mids = second.shape[0] - 1
    span = shifted.shape[1] - 256
    odd[0] = jnp.zeros(odd.shape[1:], odd.dtype)
    second[0] = jnp.zeros(second.shape[1:], second.dtype)
    for i in range(4):
        shifted[i] = stem_ref[8 - 2 * i : 8 - 2 * i + span + 256, :]

    def step(k, half):
        def stem(i):
            start = pl.multiple_of(span - 8 * k, 8)
            taps = shifted[i, pl.ds(start, 256), :].astype(jnp.bfloat16)
            return jnp.maximum(dot_nn(x_ref[...], taps), 0.0).reshape(even.shape)

        m = 2 * k + half
        even[...] = stem(2 * half)
        odd[1 - half] = stem(2 * half + 1)
        parts = (odd.at[half], even, odd.at[1 - half])
        early = jnp.zeros((main, 256), jnp.float32)
        late = jnp.zeros((rows, 256), jnp.float32)
        for df in range(3):
            src = parts[df]
            for dt in range(3):
                tap = mid_dw_ref[3 * dt + df : 3 * dt + df + 1, :]
                phase = (3, 0, 1)[dt]
                start = 7 if dt == 0 else 8
                early += src[phase, start : start + main, :] * tap
                late += src[dt + 1] * tap
        weight = mid_pw_ref[...]
        second[m + 1, 0, 8:rows, :] = jnp.maximum(dot_nn(early.astype(jnp.bfloat16), weight), 0.0)
        second[m + 1, 1] = jnp.maximum(dot_nn(late.astype(jnp.bfloat16), weight), 0.0)

    def body(k, _):
        step(k, 0)
        step(k, 1)
        return 0

    lax.fori_loop(0, mids // 2, body, 0)
    for f in range(mids // 2):
        total = jnp.zeros((main, 256), jnp.float32)
        for df in range(3):
            for dt in range(3):
                tap = last_dw_ref[3 * dt + df : 3 * dt + df + 1, :]
                phase = (1, 0, 1)[dt]
                start = 7 if dt == 0 else 8
                total += second[2 * f + df, phase, start : start + main, :] * tap
        out = jnp.maximum(dot_nn(total.astype(jnp.bfloat16), last_pw_ref[...]), 0.0)
        flat_ref[:, f * 256 : (f + 1) * 256] = out.astype(jnp.bfloat16)


def subsample(features, halo, stem_kernel, mid_depthwise, mid_pointwise, last_depthwise, last_pointwise):
    feat_rows, mel = features.shape
    main = feat_rows // 8
    rows = main + 8
    channels = stem_kernel.shape[-1]
    mids = mel // 4
    series = jnp.concatenate([jnp.zeros((56, mel), features.dtype), halo, features], axis=0)
    series = jnp.pad(series, ((0, 0), (1, MEL_PITCH - mel - 1)))
    late = jnp.pad(series, ((1, 0), (0, 0)))[:-1].reshape(rows, 8 * MEL_PITCH)
    tail = series.reshape(rows, 8 * MEL_PITCH)[:, 7 * MEL_PITCH :]
    wide = jnp.concatenate([late, tail], axis=1)
    x = jnp.concatenate(
        [wide[:, 2 * p * MEL_PITCH : (2 * p + 3) * MEL_PITCH] for p in range(4)], axis=0
    )
    x = jnp.pad(x, ((0, 0), (0, 256 - 3 * MEL_PITCH)))
    base = jnp.pad(stem_kernel.astype(jnp.float32), ((0, 0), (0, MEL_PITCH - 3), (0, 0)))
    base = base.reshape(3 * MEL_PITCH, channels)
    base = jnp.pad(base, ((mel + 8, 256 - 3 * MEL_PITCH), (0, 0)))
    return pl.pallas_call(
        subsample_kernel,
        out_shape=jax.ShapeDtypeStruct((main, (mids // 2) * channels), jnp.bfloat16),
        in_specs=[pl.BlockSpec(memory_space=pltpu.VMEM)] * 6,
        out_specs=pl.BlockSpec(memory_space=pltpu.VMEM),
        scratch_shapes=[
            pltpu.VMEM((4, rows, channels), jnp.float32),
            pltpu.VMEM((2, 4, rows, channels), jnp.float32),
            pltpu.VMEM((mids + 1, 2, rows, channels), jnp.float32),
            pltpu.VMEM((4, mel + 256, channels), jnp.float32),
        ],
        compiler_params=pltpu.CompilerParams(vmem_limit_bytes=40 * 1024 * 1024),
        cost_estimate=pl.CostEstimate(
            flops=20_000_000_000, bytes_accessed=2_000_000, transcendentals=0
        ),
        name="subsample",
    )(
        x,
        base,
        mid_depthwise.reshape(9, channels).astype(jnp.float32),
        mid_pointwise,
        last_depthwise.reshape(9, channels).astype(jnp.float32),
        last_pointwise,
    )


def forward_kernel(own, q_ref, k_ref, v_ref, do_ref, bias_ref, out_ref, stat_ref):
    scores = dot_nt(k_ref[...], q_ref[...]) * SCALE + bias_ref[...]
    top = jnp.max(scores, axis=0, keepdims=True)
    weights = jnp.exp(scores - top)
    total = jnp.sum(weights, axis=0, keepdims=True)
    probs = (weights / total).astype(jnp.bfloat16)
    out = dot_tn(probs, v_ref[...])
    out_ref[...] = out.astype(jnp.bfloat16)
    stat_ref[0, 0:1, :] = top + jnp.log(total)
    prod = do_ref[...].astype(jnp.float32) * out
    stat_ref[0, 1:2, :] = jnp.sum(prod.T, axis=0, keepdims=True)


def backward_kernel(own, q_ref, k_ref, v_ref, do_ref, stat_ref, bias_ref, bias2_ref, dq_ref, dk_ref, dv_ref):
    rows = own.stop - own.start
    blocks = q_ref.shape[0] // rows
    q_own, k_own, v_own, do_own = (r[own, :] for r in (q_ref, k_ref, v_ref, do_ref))
    mid = blocks // 2
    log_norm = stat_ref[mid, 0, 0:1, :]
    delta = stat_ref[mid, 0, 1:2, :]
    weights = jnp.exp(dot_nt(k_ref[...], q_own) * SCALE + bias_ref[...] - log_norm)
    dscore = (weights * (dot_nt(v_ref[...], do_own) - delta)).astype(jnp.bfloat16)
    dq_ref[...] = (dot_tn(dscore, k_ref[...]) * SCALE).astype(jnp.bfloat16)
    log_norms = jnp.concatenate([stat_ref[b, 0, 0:1, :] for b in range(blocks)], axis=1)
    deltas = jnp.concatenate([stat_ref[b, 0, 1:2, :] for b in range(blocks)], axis=1)
    weights2 = jnp.exp(dot_nt(k_own, q_ref[...]) * SCALE + bias2_ref[...] - log_norms)
    dscore2 = (weights2 * (dot_nt(v_own, do_ref[...]) - deltas)).astype(jnp.bfloat16)
    dk_ref[...] = (dot_nn(dscore2, q_ref[...]) * SCALE).astype(jnp.bfloat16)
    dv_ref[...] = dot_nn(weights2.astype(jnp.bfloat16), do_ref[...]).astype(jnp.bfloat16)


def attention_forward(projected, d_attention, bias, rows):
    window = projected.shape[0]
    width = HEADS * HEAD_DIM
    own = slice(REACH * rows, (REACH + 1) * rows)
    return pl.pallas_call(
        functools.partial(forward_kernel, own),
        grid=(HEADS,),
        out_shape=(
            jax.ShapeDtypeStruct((rows, width), jnp.bfloat16),
            jax.ShapeDtypeStruct((HEADS, 2, rows), jnp.float32),
        ),
        in_specs=[
            pl.BlockSpec((rows, HEAD_DIM), lambda h: (REACH, h)),
            pl.BlockSpec((window, HEAD_DIM), lambda h: (0, HEADS + h)),
            pl.BlockSpec((window, HEAD_DIM), lambda h: (0, 2 * HEADS + h)),
            pl.BlockSpec((rows, HEAD_DIM), lambda h: (REACH, h)),
            pl.BlockSpec((window, rows), lambda h: (0, 0)),
        ],
        out_specs=(
            pl.BlockSpec((rows, HEAD_DIM), lambda h: (0, h)),
            pl.BlockSpec((1, 2, rows), lambda h: (h, 0, 0)),
        ),
        name="attention_forward",
    )(projected, projected, projected, d_attention, bias)


def attention_backward(projected, d_attention, stats, bias, bias2, rows):
    window = projected.shape[0]
    width = HEADS * HEAD_DIM
    own = slice(REACH * rows, (REACH + 1) * rows)
    grad = jax.ShapeDtypeStruct((rows, width), jnp.bfloat16)
    return pl.pallas_call(
        functools.partial(backward_kernel, own),
        grid=(HEADS,),
        out_shape=(grad, grad, grad),
        in_specs=[
            pl.BlockSpec((window, HEAD_DIM), lambda h: (0, h)),
            pl.BlockSpec((window, HEAD_DIM), lambda h: (0, HEADS + h)),
            pl.BlockSpec((window, HEAD_DIM), lambda h: (0, 2 * HEADS + h)),
            pl.BlockSpec((window, HEAD_DIM), lambda h: (0, h)),
            pl.BlockSpec((2 * REACH + 1, 1, 2, rows), lambda h: (0, h, 0, 0)),
            pl.BlockSpec((window, rows), lambda h: (0, 0)),
            pl.BlockSpec((rows, window), lambda h: (0, 0)),
        ],
        out_specs=(pl.BlockSpec((rows, HEAD_DIM), lambda h: (0, h)),) * 3,
        name="attention_backward",
    )(projected, projected, projected, d_attention, stats, bias, bias2)


def gathered_window(x, size):
    def moved(value, pairs):
        return lax.ppermute(value, "tm", pairs)

    swap = [(i, i ^ 1) for i in range(size)]
    before = moved(x, [(i, i + 2) for i in range(size - 2)])
    after = moved(x, [(i, i - 2) for i in range(2, size)])
    far = [(i, i + 3) for i in range(1, size, 2) if i + 3 < size]
    far += [(i, i - 3) for i in range(0, size, 2) if i - 3 >= 0]
    far_block = moved(x, far)
    sibling = moved(x, swap)
    sib_before = moved(before, swap)
    sib_after = moved(after, swap)
    is_even = lax.axis_index("tm") % 2 == 0

    def pick(a, b):
        return jnp.where(is_even, a, b)

    return [
        pick(far_block, sib_before),
        before,
        pick(sib_before, sibling),
        x,
        pick(sibling, sib_after),
        after,
        pick(sib_after, far_block),
    ]


def segment_of(positions, utt_bounds):
    inside = (utt_bounds[None, :, 0] <= positions[:, None]) & (
        positions[:, None] < utt_bounds[None, :, 1]
    )
    number = jnp.arange(utt_bounds.shape[0], dtype=jnp.int32)
    found = jnp.sum(jnp.where(inside, number[None, :], 0), axis=1)
    return jnp.where(jnp.any(inside, axis=1), found, -1)


def per_device(
    size,
    features,
    stem_kernel,
    mid_depthwise,
    mid_pointwise,
    last_depthwise,
    last_pointwise,
    proj_weight,
    norm_gain,
    qkv_weight,
    out_weight,
    cotangent,
    utt_bounds,
    live_blocks,
):
    rows = cotangent.shape[0]
    window = (2 * REACH + 1) * rows
    halo = lax.ppermute(features[-8:], "tm", [(i, i + 1) for i in range(size - 1)])
    flat_rows = subsample(
        features, halo, stem_kernel, mid_depthwise, mid_pointwise, last_depthwise, last_pointwise
    )
    cot_window = jnp.concatenate(gathered_window(cotangent, size), axis=0)
    d_attention = dot_nt(cot_window, out_weight).astype(jnp.bfloat16)

    my_index = lax.axis_index("tm")
    local_seg = segment_of(my_index * rows + jnp.arange(rows, dtype=jnp.int32), utt_bounds)
    window_seg = segment_of(
        (my_index - REACH) * rows + jnp.arange(window, dtype=jnp.int32), utt_bounds
    )
    flag = jnp.repeat(live_blocks[0], rows, total_repeat_length=window)
    bias = jnp.where(
        (window_seg[:, None] == local_seg[None, :]) & (flag[:, None] == 1), 0.0, neg_fill
    )
    bias2 = jnp.where(
        (local_seg[:, None] == window_seg[None, :]) & (flag[None, :] == 1), 0.0, neg_fill
    )

    frames = dot_nn(flat_rows, proj_weight).astype(jnp.bfloat16)
    frames_f = frames.astype(jnp.float32)
    row_mean = jnp.mean(frames_f, axis=-1, keepdims=True)
    centered = frames_f - row_mean
    inv_std = lax.rsqrt(jnp.mean(centered * centered, axis=-1, keepdims=True) + norm_eps)
    normalized = centered * inv_std
    normed = (normalized * norm_gain).astype(jnp.bfloat16)
    normed_window = jnp.concatenate(gathered_window(normed, size), axis=0)
    projected = dot_nn(normed_window, qkv_weight).astype(jnp.bfloat16)
    attention, stats = attention_forward(projected, d_attention, bias, rows)
    stats_window = jnp.stack(gathered_window(stats, size), axis=0)
    block_out = (frames_f + dot_nn(attention, out_weight)).astype(jnp.bfloat16)
    grads = attention_backward(projected, d_attention, stats_window, bias, bias2, rows)
    width = cotangent.shape[1]
    grad_normed = sum(
        dot_nt(g, qkv_weight[:, i * width : (i + 1) * width]) for i, g in enumerate(grads)
    )
    scaled_grad = grad_normed * norm_gain
    ln_grad = inv_std * (
        scaled_grad
        - jnp.mean(scaled_grad, axis=-1, keepdims=True)
        - normalized * jnp.mean(scaled_grad * normalized, axis=-1, keepdims=True)
    )
    frame_grads = (cotangent.astype(jnp.float32) + ln_grad).astype(jnp.bfloat16)
    own_cols = size * (flat_rows.shape[1] // size)
    columns = lax.all_to_all(flat_rows[:, :own_cols], "tm", 1, 0, tiled=True)
    all_grads = lax.all_gather(frame_grads, "tm", axis=0, tiled=True)
    proj_grads = dot_tn(columns, all_grads)
    return (block_out, frame_grads, proj_grads)


def solution(mesh):
    split = P(("groups", "tm"), None)
    in_specs = (split,) + (P(),) * 9 + (split, P("groups", None), split)
    return jax.shard_map(
        functools.partial(per_device, mesh.shape["tm"]),
        mesh=mesh,
        in_specs=in_specs,
        out_specs=(split, split, split),
        check_vma=False,
    )
```

time: 389 us -> 204 us (0.52); the launches traced: 383 us -> 202 us
  local copies, waits for them, and re-layouts: 104 us -> 18.2 us
  waiting for transfers between devices: 102 us -> 55.9 us
  starting transfers between devices: 86 us -> 42.5 us
  Pallas kernels: 0 us -> 32.4 us
  matrix products: 52.3 us -> 24.6 us
  other arithmetic: 23.5 us -> 14.1 us
    reduce_scatter x1 -> x0, waiting for transfers between devices: 88.2 us -> none  [per_device(): lax.psum_scatter(lax.dot_general(flat_cols, frame_grads, (((0,), (0,)), (...]
    ppermute x15 -> x19, starting transfers between devices: 86 us -> 37.7 us  [the longest x18 35.8 us: moved(): return lax.ppermute(value, 'tm', pairs)]
    conv_general_dilated x7 -> x0, local copies, waits for them, and re-layouts: 42.6 us -> none  [conv_valid(): lax.conv_general_dilated(inputs[None], kernel, (2, 2), ((0, 0), (1, 1)),...]
    convert_element_type x16 -> x2, local copies, waits for them, and re-layouts: 36.6 us -> 1.41 us  [the longest x1 0.7 us: subsample(): mid_depthwise.reshape(9, channels).astype(jnp.float32)]
    pallas_call x0 -> x3, Pallas kernels: none -> 32.4 us  [the longest x1 12.5 us: subsample(): pl.pallas_call(subsample_kernel, out_shape=jax.ShapeDtypeStruct((main, mi...]
    all_gather x0 -> x1, waiting for transfers between devices: none -> 28.8 us  [per_device(): all_grads = lax.all_gather(frame_grads, 'tm', axis=0, tiled=True)]
    all_to_all x0 -> x1, waiting for transfers between devices: none -> 23.4 us  [per_device(): columns = lax.all_to_all(flat_rows[:, :own_cols], 'tm', 1, 0, tiled=True)]
    conv_general_dilated x3 -> x0, matrix products: 22.5 us -> none  [conv_valid(): lax.conv_general_dilated(inputs[None], kernel, (2, 2), ((0, 0), (1, 1)),...]
  transfers between devices with their start and end apart: 16 -> 21, of which waited for: 6 -> 4; matrix products, arithmetic and copies ran while one was open for 7% -> 14% of each run, Pallas kernels for 0% -> 6%
where the time goes in v1:
time: 204 us; the launch traced here: 202 us
  waiting for transfers between devices  55.9 us (27%)
  starting transfers between devices  42.5 us (21%)
  Pallas kernels  32.4 us (16%)
  matrix products  24.6 us (12%)
  local copies, waits for them, and re-layouts  18.2 us (9%)
  between operations  14.6 us (7%)
  other arithmetic  14.1 us (7%)
    ppermute x18, starting transfers between devices, moved(): return lax.ppermute(value, 'tm', pairs)  35.8 us
    all_gather x1, waiting for transfers between devices, per_device(): all_grads = lax.all_gather(frame_grads, 'tm', axis=0, tiled=True)  28.8 us
    all_to_all x1, waiting for transfers between devices, per_device(): columns = lax.all_to_all(flat_rows[:, :own_cols], 'tm', 1, 0, tiled=True)  23.4 us
    pallas_call x1, Pallas kernels, subsample(): pl.pallas_call(subsample_kernel, out_shape=jax.ShapeDtypeStruct((main, mi...  12.5 us
    dot_general x4, matrix products, dot_nt(): lax.dot_general(a, b, (((1,), (1,)), ((), ())), preferred_element_type=jn...  10.9 us
    pallas_call x1, Pallas kernels, attention_backward(): pl.pallas_call(functools.partial(backward_kernel, own), grid=(HEADS,), ou...  10.6 us
    dot_general x3, matrix products, dot_nn(): return jnp.dot(a, b, preferred_element_type=jnp.float32)  9.82 us
    pallas_call x1, Pallas kernels, attention_forward(): pl.pallas_call(functools.partial(forward_kernel, own), grid=(HEADS,), out...  9.27 us
  transfers between devices with their start and end apart: 21, of which 4 were waited for; matrix products, arithmetic and copies ran while one was open for 14% of the time, Pallas kernels for 6%

profile of v1, /device:TPU:0, one launch (start us, length us, event | category | flops | bytes accessed | tf_op | source)
XLA Modules:
  0.0 202.4 jit_solution(13429129492682706127)
XLA Ops:
  7.2 5.7 %collective-permute-start.8 = (bf16[128,1024]{1,0:T(8,128)(2,1)}, bf16[128,1024]{1,0:T(8,128)(2,1)}, u32[]{:S(2)}, u32[]{:S(2)}) collective-permute-start(bf16[128,1024]{1,0:T(8,128)(2,1)} %param.25), channel_id=1, source_target_pairs={{0,2},{1,3},{2,4},{3,5},{4,6},{5,7},{6,8},{7,9},{8,10},{9,11},{10,... | collective-permute-start | bytes 786440 | tf_op jit(solution)/shard_map/ppermute | solution.py:211
  12.9 1.4 collective-permute-start.7
  14.3 1.6 collective-permute-start.10
  15.9 1.3 collective-permute-start.11
  17.2 0.8 slice.54
  18.0 1.9 collective-permute-start
  20.0 0.8 slice_bitcast_fusion.1
  21.1 0.7 pad.29
  21.8 1.6 fusion.41
  23.4 4.6 %fusion.37 = s32[896]{0:T(1024)S(1)} fusion(s32[1,1,7,128]{3,2,1,0:T(8,128)S(1)} %get-tuple-element.45, s32[1,1,7,128]{3,2,1,0:T(8,128)S(1)} %get-tuple-element.44, s32[]{:T(128)} %bitcast.4, s32[]{:T(128)} %bitcast.5, s32[]{:T(128)} %bitcast.6, s32[]{:T(128)} %bitcast.7, s32[]{:T(128)} %bitcast.8, s32[]{:T(128)} %bitcast.10, s32[]{:T(128)} %bitcast.9), kind=kLoop, calls=%fused_computation.81 | loop fusion | flops 12544 | bytes 10780 | tf_op jit(solution)/shard_map/jit(_take)/gather | solution.py:277
  28.1 1.1 and_select_fusion.1.bias_ref
  29.2 0.7 reshape.189.mid_dw_ref
  29.9 0.7 reshape.190.last_dw_ref
  30.6 1.1 concatenate.19
  31.8 0.8 pad_slice_fusion
  32.6 0.2 copy.23
  32.8 1.8 copy.22
  34.6 1.2 reshape.186
  36.0 0.9 reshape.187
  36.9 1.1 slice.85
  38.1 12.5 %subsample.1 = bf16[128,2560]{1,0:T(8,128)(2,1)S(1)} custom-call(bf16[544,256]{1,0:T(8,128)(2,1)S(1)} %fusion.27.x_ref, f32[344,256]{1,0:T(8,128)S(1)} %pad_convert_fusion.stem_ref, f32[9,256]{1,0:T(8,128)S(1)} %reshape.189.mid_dw_ref, bf16[256,256]{1,0:T(8,128)(2,1)S(1)} %copy-done.1, f32[9,256]{1,0:T(8,128)S(1)} %reshape.190.last_dw_ref, ...), custom_call_target="tpu_custom_call" | custom-call | flops 20000000000 | bytes 2000000 | tf_op jit(solution)/shard_map/subsample/pallas_call | solution.py:103
  50.7 0.9 fusion.42
  51.6 0.2 multiply_reduce_fusion.1
  51.8 2.8 %collective-permute-start.9 = (bf16[128,1024]{1,0:T(8,128)(2,1)}, bf16[128,1024]{1,0:T(8,128)(2,1)S(1)}, u32[]{:S(2)}, u32[]{:S(2)}) collective-permute-start(bf16[128,1024]{1,0:T(8,128)(2,1)} %collective-permute-done.8), channel_id=1, source_target_pairs={{0,1},{1,0},{2,3},{3,2},{4,5},{5,4},{6,7},{7,6},{8,9},{9,8},{10,11... | collective-permute-start | bytes 786440 | tf_op jit(solution)/shard_map/ppermute | solution.py:211
  54.6 0.1 multiply_convert_fusion
  54.8 4.5 %collective-permute-start.2 = (bf16[128,1024]{1,0:T(8,128)(2,1)S(1)}, bf16[128,1024]{1,0:T(8,128)(2,1)S(1)}, u32[]{:S(2)}, u32[]{:S(2)}) collective-permute-start(bf16[128,1024]{1,0:T(8,128)(2,1)S(1)} %multiply_convert_fusion), channel_id=1, source_target_pairs={{0,2},{1,3},{2,4},{3,5},{4,6},{5,7},{6,8},{7,9},{8,10},{9,11},{10,... | collective-permute-start | bytes 786440 | tf_op jit(solution)/shard_map/ppermute | solution.py:211
  59.3 0.7 collective-permute-start.1
  60.0 1.5 collective-permute-start.5
  61.5 1.0 select_dynamic-update-slice_fusion.3
  62.5 1.0 constant_dynamic-update-slice_fusion.5
  63.5 2.0 %collective-permute-start.4 = (bf16[128,1024]{1,0:T(8,128)(2,1)S(1)}, bf16[128,1024]{1,0:T(8,128)(2,1)S(1)}, u32[]{:S(2)}, u32[]{:S(2)}) collective-permute-start(bf16[128,1024]{1,0:T(8,128)(2,1)S(1)} %multiply_convert_fusion), channel_id=1, source_target_pairs={{0,1},{1,0},{2,3},{3,2},{4,5},{5,4},{6,7},{7,6},{8,9},{9,8},{10,11... | collective-permute-start | bytes 786440 | tf_op jit(solution)/shard_map/ppermute | solution.py:211
  65.6 0.4 collective-permute-start.3
  66.0 3.0 %collective-permute-done.5 = bf16[128,1024]{1,0:T(8,128)(2,1)S(1)} collective-permute-done((bf16[128,1024]{1,0:T(8,128)(2,1)S(1)}, bf16[128,1024]{1,0:T(8,128)(2,1)S(1)}, u32[]{:S(2)}, u32[]{:S(2)}) %collective-permute-start.5) | collective-permute-done | bytes 262176 | tf_op jit(solution)/shard_map/ppermute | solution.py:211
  69.0 1.8 collective-permute-start.6
  71.4 0.7 collective-permute-done.6
  72.0 1.1 select_dynamic-update-slice_fusion.1
  73.3 7.7 %convolution_convert_fusion.q_ref.k_ref.v_ref = bf16[896,3072]{1,0:T(8,128)(2,1)} fusion(bf16[896,1024]{1,0:T(8,128)(2,1)S(1)} %select_dynamic-update-slice_fusion.4, bf16[1024,3072]{1,0:T(8,128)(2,1)S(1)} %bitcast.86), kind=kOutput, calls=%fused_computation | convolution fusion | flops 5639897088 | bytes 13631488 | tf_op jit(solution)/shard_map/dot_general | solution.py:28
  81.1 1.0 constant_dynamic-update-slice_fusion.3
  82.1 3.4 %convolution_convert_fusion.1.do_ref = bf16[896,1024]{1,0:T(8,128)(2,1)} fusion(bf16[896,1024]{1,0:T(8,128)(2,1)S(1)} %select_dynamic-update-slice_fusion, bf16[1024,1024]{1,0:T(8,128)(2,1)S(1)} %copy-done), kind=kOutput, calls=%fused_computation.7 | convolution fusion | flops 1879965696 | bytes 5767168 | tf_op jit(solution)/shard_map/dot_general | solution.py:20
  85.5 9.3 %attention_forward.1 = (bf16[128,1024]{1,0:T(8,128)(2,1)}, f32[8,2,128]{2,1,0:T(2,128)}) custom-call(bf16[896,3072]{1,0:T(8,128)(2,1)} %convolution_convert_fusion.q_ref.k_ref.v_ref, bf16[896,3072]{1,0:T(8,128)(2,1)} %convolution_convert_fusion.q_ref.k_ref.v_ref, bf16[896,3072]{1,0:T(8,128)(2,1)} %convolution_convert_fusion.q_ref.k_ref.v_ref, ...), custom_call_target="tpu_custom_call" | custom-call | tf_op jit(solution)/shard_map/attention_forward/pallas_call | solution.py:164
  94.7 5.2 %collective-permute-start.14 = (f32[8,2,128]{2,1,0:T(2,128)}, f32[8,2,128]{2,1,0:T(2,128)S(1)}, u32[]{:S(2)}, u32[]{:S(2)}) collective-permute-start(f32[8,2,128]{2,1,0:T(2,128)} %get-tuple-element.21), channel_id=1, source_target_pairs={{0,2},{1,3},{2,4},{3,5},{4,6},{5,7},{6,8},{7,9},{8,10},{9,11},{10,... | collective-permute-start | bytes 24584 | tf_op jit(solution)/shard_map/ppermute | solution.py:211
  99.9 0.7 collective-permute-start.13
  100.6 1.3 collective-permute-start.17
  101.9 3.2 %collective-permute-start.15 = (f32[8,2,128]{2,1,0:T(2,128)S(1)}, f32[8,2,128]{2,1,0:T(2,128)S(1)}, u32[]{:S(2)}, u32[]{:S(2)}) collective-permute-start(f32[8,2,128]{2,1,0:T(2,128)S(1)} %collective-permute-done.14), channel_id=1, source_target_pairs={{0,1},{1,0},{2,3},{3,2},{4,5},{5,4},{6,7},{7,6},{8,9},{9,8},{10,11... | collective-permute-start | bytes 24584 | tf_op jit(solution)/shard_map/ppermute | solution.py:211
  105.1 1.5 and_select_fusion.bias2_ref
  106.6 1.7 collective-permute-start.18
  108.3 0.6 constant_dynamic-update-slice_fusion.12
  109.0 0.6 constant_dynamic-update-slice_fusion.11
  109.5 0.6 constant_dynamic-update-slice_fusion.10
  110.2 1.3 constant_dynamic-update-slice_fusion.9
  111.4 0.6 constant_dynamic-update-slice_fusion.8
  112.1 0.6 constant_dynamic-update-slice_fusion.7
  112.6 0.6 constant_dynamic-update-slice_fusion.6.stat_ref
  113.2 10.6 %attention_backward.1 = (bf16[128,1024]{1,0:T(8,128)(2,1)}, bf16[128,1024]{1,0:T(8,128)(2,1)}, bf16[128,1024]{1,0:T(8,128)(2,1)}) custom-call(bf16[896,3072]{1,0:T(8,128)(2,1)} %convolution_convert_fusion.q_ref.k_ref.v_ref, bf16[896,3072]{1,0:T(8,128)(2,1)} %convolution_convert_fusion.q_ref.k_ref.v_ref, ...), custom_call_target="tpu_custom_call" | custom-call | tf_op jit(solution)/shard_map/attention_backward/pallas_call | solution.py:191
  123.9 2.5 %fusion = f32[128,1024]{1,0:T(8,128)S(1)} fusion(bf16[128,1024]{1,0:T(8,128)(2,1)} %get-tuple-element.24, bf16[1024,3072]{1,0:T(8,128)(2,1)} %param.23), kind=kOutput, calls=%fused_computation.1 | convolution fusion | flops 268435456 | bytes 2883584 | tf_op jit(solution)/shard_map/dot_general | solution.py:20
  126.4 2.5 %fusion.2 = f32[128,1024]{1,0:T(8,128)S(1)} fusion(bf16[128,1024]{1,0:T(8,128)(2,1)S(1)} %copy-done.10, bf16[1024,3072]{1,0:T(8,128)(2,1)} %param.23), kind=kOutput, calls=%fused_computation.3 | convolution fusion | flops 268435456 | bytes 2883584 | tf_op jit(solution)/shard_map/dot_general | solution.py:20
  128.9 2.6 %fusion.39 = (f32[128]{0:T(128)S(1)}, f32[128]{0:T(128)S(1)}, f32[128,1024]{1,0:T(8,128)S(1)}) fusion(f32[128]{0:T(128)S(1)} %copy-done.8, f32[128,1024]{1,0:T(8,128)S(1)} %get-tuple-element.40, f32[128]{0:T(128)S(1)} %broadcast_multiply_fusion.2, f32[1024]{0:T(1024)S(1)} %copy-done.6, f32[128,1024]{1,0:T(8,128)S(1)} %fusion, f32[128,1024]{1,0:T(8,128)S(1)} %fusion.2, ...), kind=kOutput, calls=%fused_computation.92 | convolution fusion | flops 269483776 | bytes 4462592 | tf_op jit(solution)/shard_map/dot_general | solution.py:20
  131.5 1.0 add_convert_fusion
  132.5 1.1 copy.24
  133.6 4.7 %all-to-all-start = ((bf16[128,16,160]{0,2,1:T(8,128)(2,1)}), bf16[128,16,160]{0,2,1:T(8,128)(2,1)S(1)}, u32[]{:S(2)}, u32[]{:S(2)}) async-start(bf16[128,16,160]{0,2,1:T(8,128)(2,1)} %bitcast.84), calls=%async_computation | async-start | bytes 1310720 | tf_op jit(solution)/shard_map/all_to_all | solution.py:310
  138.4 1.2 fusion.16
  139.5 23.4 %all-to-all-done = bf16[128,16,160]{0,2,1:T(8,128)(2,1)S(1)} async-done(((bf16[128,16,160]{0,2,1:T(8,128)(2,1)}), bf16[128,16,160]{0,2,1:T(8,128)(2,1)S(1)}, u32[]{:S(2)}, u32[]{:S(2)}) %all-to-all-start) | async-done | bytes 655392 | tf_op jit(solution)/shard_map/all_to_all | solution.py:310
  162.9 28.8 %all-gather.2.cloned.1.call-done = bf16[2048,1024]{1,0:T(8,128)(2,1)} async-done(((bf16[128,1024]{1,0:T(8,128)(2,1)}), bf16[2048,1024]{1,0:T(8,128)(2,1)}) %all-gather.2.cloned.1.call-update) | async-done | bytes 4194320 | tf_op jit(solution)/shard_map/all_gather | solution.py:311
  191.6 3.9 %fusion.17 = f32[160,1024]{1,0:T(8,128)} fusion(bf16[2048,1024]{1,0:T(8,128)(2,1)} %all-gather.2.cloned.1.call-done, bf16[128,16,160]{0,2,1:T(8,128)(2,1)S(1)} %all-to-all-done), kind=kOutput, calls=%fused_computation.15 | convolution fusion | flops 671088640 | bytes 5505024 | tf_op jit(solution)/shard_map/dot_general | solution.py:24
  (82 shorter events, 1.6 us)
Async XLA Ops:
  7.2 74.9 %copy-start = (bf16[1024,1024]{1,0:T(8,128)(2,1)S(1)}, bf16[1024,1024]{1,0:T(8,128)(2,1)}, u32[]{:S(2)}) copy-start(bf16[1024,1024]{1,0:T(8,128)(2,1)} %param.24) | copy-start | bytes 6291460
  7.2 184.5 %all-gather.2.cloned.1.call-start = ((), (), s32[]{:S(2)}) async-start(), calls=%async_computation.1 | async-start | bytes 4456448 | tf_op jit(solution)/shard_map/all_gather | solution.py:311
  7.2 44.6 %collective-permute-start.8 = (bf16[128,1024]{1,0:T(8,128)(2,1)}, bf16[128,1024]{1,0:T(8,128)(2,1)}, u32[]{:S(2)}, u32[]{:S(2)}) collective-permute-start(bf16[128,1024]{1,0:T(8,128)(2,1)} %param.25), channel_id=1, source_target_pairs={{0,2},{1,3},{2,4},{3,5},{4,6},{5,7},{6,8},{7,9},{8,10},{9,11},{10,... | collective-permute-start | bytes 786440 | tf_op jit(solution)/shard_map/ppermute | solution.py:211
  12.9 46.3 %collective-permute-start.7 = (bf16[128,1024]{1,0:T(8,128)(2,1)}, bf16[128,1024]{1,0:T(8,128)(2,1)}, u32[]{:S(2)}, u32[]{:S(2)}) collective-permute-start(bf16[128,1024]{1,0:T(8,128)(2,1)} %param.25), channel_id=1, source_target_pairs={{1,4},{3,6},{5,8},{7,10},{9,12},{11,14},{4,1},{6,3},{8,5},{10,7},{... | collective-permute-start | bytes 786440 | tf_op jit(solution)/shard_map/ppermute | solution.py:211
  14.3 49.2 %collective-permute-start.10 = (bf16[128,1024]{1,0:T(8,128)(2,1)}, bf16[128,1024]{1,0:T(8,128)(2,1)}, u32[]{:S(2)}, u32[]{:S(2)}) collective-permute-start(bf16[128,1024]{1,0:T(8,128)(2,1)} %param.25), channel_id=1, source_target_pairs={{0,1},{1,0},{2,3},{3,2},{4,5},{5,4},{6,7},{7,6},{8,9},{9,8},{10,11... | collective-permute-start | bytes 786440 | tf_op jit(solution)/shard_map/ppermute | solution.py:211
  15.9 49.6 %collective-permute-start.11 = (bf16[128,1024]{1,0:T(8,128)(2,1)}, bf16[128,1024]{1,0:T(8,128)(2,1)}, u32[]{:S(2)}, u32[]{:S(2)}) collective-permute-start(bf16[128,1024]{1,0:T(8,128)(2,1)} %param.25), channel_id=1, source_target_pairs={{2,0},{3,1},{4,2},{5,3},{6,4},{7,5},{8,6},{9,7},{10,8},{11,9},{12,... | collective-permute-start | bytes 786440 | tf_op jit(solution)/shard_map/ppermute | solution.py:211
  18.0 12.6 %collective-permute-start = (bf16[8,80]{0,1:T(8,128)(2,1)S(1)}, bf16[8,80]{0,1:T(8,128)(2,1)S(1)}, u32[]{:S(2)}, u32[]{:S(2)}) collective-permute-start(bf16[8,80]{0,1:T(8,128)(2,1)S(1)} %slice.54), channel_id=1, source_target_pairs={{0,1},{1,2},{2,3},{3,4},{4,5},{5,6},{6,7},{7,8},{8,9},{9,10},{10,1... | collective-permute-start | bytes 3848 | tf_op jit(solution)/shard_map/ppermute | solution.py:265
  28.1 7.9 %copy-start.9 = (s32[128]{0:T(128)}, s32[128]{0:T(128)S(1)}, u32[]{:S(2)}) copy-start(s32[128]{0:T(128)S(1)} %broadcast_select_fusion.1) | copy-start | bytes 1540
  31.8 6.3 %copy-start.1 = (bf16[256,256]{1,0:T(8,128)(2,1)S(1)}, bf16[256,256]{1,0:T(8,128)(2,1)}, u32[]{:S(2)}) copy-start(bf16[256,256]{1,0:T(8,128)(2,1)} %mid_pw_ref.1) | copy-start | bytes 393220
  31.8 6.3 %copy-start.2 = (bf16[256,256]{1,0:T(8,128)(2,1)S(1)}, bf16[256,256]{1,0:T(8,128)(2,1)}, u32[]{:S(2)}) copy-start(bf16[256,256]{1,0:T(8,128)(2,1)} %last_pw_ref.1) | copy-start | bytes 393220
  36.9 13.8 %slice-start = ((s8[5242880]{0:T(1024)(128)(4,1)}), s8[4194304]{0:T(1024)(128)(4,1)S(1)}, s32[]{:S(2)}) async-start(s8[5242880]{0:T(1024)(128)(4,1)} %bitcast.82), calls=%async_computation.2 | async-start | bytes 8388608
  38.1 12.5 %slice-start.1 = ((s8[5242880]{0:T(1024)(128)(4,1)}), s8[1048576]{0:T(1024)(128)(4,1)S(1)}, s32[]{:S(2)}) async-start(s8[5242880]{0:T(1024)(128)(4,1)} %bitcast.82), calls=%async_computation.3 | async-start | bytes 2097152
  50.6 4.0 %copy-start.6 = (f32[1024]{0:T(1024)S(1)}, f32[1024]{0:T(1024)}, u32[]{:S(2)}) copy-start(f32[1024]{0:T(1024)} %param.22) | copy-start | bytes 12292
  50.7 22.6 %slice-start.2 = ((s8[6291456]{0:T(1024)(128)(4,1)}), s8[4194304]{0:T(1024)(128)(4,1)S(1)}, s32[]{:S(2)}) async-start(s8[6291456]{0:T(1024)(128)(4,1)} %bitcast.85), calls=%async_computation.4 | async-start | bytes 8388608
  51.6 19.4 %copy-start.3 = (bf16[128,1024]{1,0:T(8,128)(2,1)S(1)}, bf16[128,1024]{1,0:T(8,128)(2,1)}, u32[]{:S(2)}) copy-start(bf16[128,1024]{1,0:T(8,128)(2,1)} %param.25) | copy-start | bytes 786436
  51.8 8.1 %collective-permute-start.9 = (bf16[128,1024]{1,0:T(8,128)(2,1)}, bf16[128,1024]{1,0:T(8,128)(2,1)S(1)}, u32[]{:S(2)}, u32[]{:S(2)}) collective-permute-start(bf16[128,1024]{1,0:T(8,128)(2,1)} %collective-permute-done.8), channel_id=1, source_target_pairs={{0,1},{1,0},{2,3},{3,2},{4,5},{5,4},{6,7},{7,6},{8,9},{9,8},{10,11... | collective-permute-start | bytes 786440 | tf_op jit(solution)/shard_map/ppermute | solution.py:211
  54.6 16.6 %copy-start.7 = (f32[128]{0:T(128)}, f32[128]{0:T(128)S(1)}, u32[]{:S(2)}) copy-start(f32[128]{0:T(128)S(1)} %add_rsqrt_fusion) | copy-start | bytes 1540
  54.8 18.5 %slice-start.3 = ((s8[6291456]{0:T(1024)(128)(4,1)}), s8[2097152]{0:T(1024)(128)(4,1)S(1)}, s32[]{:S(2)}) async-start(s8[6291456]{0:T(1024)(128)(4,1)} %bitcast.85), calls=%async_computation.5 | async-start | bytes 4194304
  54.8 10.8 %collective-permute-start.2 = (bf16[128,1024]{1,0:T(8,128)(2,1)S(1)}, bf16[128,1024]{1,0:T(8,128)(2,1)S(1)}, u32[]{:S(2)}, u32[]{:S(2)}) collective-permute-start(bf16[128,1024]{1,0:T(8,128)(2,1)S(1)} %multiply_convert_fusion), channel_id=1, source_target_pairs={{0,2},{1,3},{2,4},{3,5},{4,6},{5,7},{6,8},{7,9},{8,10},{9,11},{10,... | collective-permute-start | bytes 786440 | tf_op jit(solution)/shard_map/ppermute | solution.py:211
  59.3 11.7 %collective-permute-start.1 = (bf16[128,1024]{1,0:T(8,128)(2,1)S(1)}, bf16[128,1024]{1,0:T(8,128)(2,1)S(1)}, u32[]{:S(2)}, u32[]{:S(2)}) collective-permute-start(bf16[128,1024]{1,0:T(8,128)(2,1)S(1)} %multiply_convert_fusion), channel_id=1, source_target_pairs={{1,4},{3,6},{5,8},{7,10},{9,12},{11,14},{4,1},{6,3},{8,5},{10,7},{... | collective-permute-start | bytes 786440 | tf_op jit(solution)/shard_map/ppermute | solution.py:211
  60.0 9.1 %collective-permute-start.5 = (bf16[128,1024]{1,0:T(8,128)(2,1)S(1)}, bf16[128,1024]{1,0:T(8,128)(2,1)S(1)}, u32[]{:S(2)}, u32[]{:S(2)}) collective-permute-start(bf16[128,1024]{1,0:T(8,128)(2,1)S(1)} %multiply_convert_fusion), channel_id=1, source_target_pairs={{2,0},{3,1},{4,2},{5,3},{6,4},{7,5},{8,6},{9,7},{10,8},{11,9},{12,... | collective-permute-start | bytes 786440 | tf_op jit(solution)/shard_map/ppermute | solution.py:211
  63.5 7.6 %collective-permute-start.4 = (bf16[128,1024]{1,0:T(8,128)(2,1)S(1)}, bf16[128,1024]{1,0:T(8,128)(2,1)S(1)}, u32[]{:S(2)}, u32[]{:S(2)}) collective-permute-start(bf16[128,1024]{1,0:T(8,128)(2,1)S(1)} %multiply_convert_fusion), channel_id=1, source_target_pairs={{0,1},{1,0},{2,3},{3,2},{4,5},{5,4},{6,7},{7,6},{8,9},{9,8},{10,11... | collective-permute-start | bytes 786440 | tf_op jit(solution)/shard_map/ppermute | solution.py:211
  65.5 5.8 %collective-permute-start.12 = (bf16[128,1024]{1,0:T(8,128)(2,1)}, bf16[128,1024]{1,0:T(8,128)(2,1)S(1)}, u32[]{:S(2)}, u32[]{:S(2)}) collective-permute-start(bf16[128,1024]{1,0:T(8,128)(2,1)} %collective-permute-done.11), channel_id=1, source_target_pairs={{0,1},{1,0},{2,3},{3,2},{4,5},{5,4},{6,7},{7,6},{8,9},{9,8},{10,11... | collective-permute-start | bytes 786440 | tf_op jit(solution)/shard_map/ppermute | solution.py:211
  65.6 5.4 %collective-permute-start.3 = (bf16[128,1024]{1,0:T(8,128)(2,1)S(1)}, bf16[128,1024]{1,0:T(8,128)(2,1)S(1)}, u32[]{:S(2)}, u32[]{:S(2)}) collective-permute-start(bf16[128,1024]{1,0:T(8,128)(2,1)S(1)} %collective-permute-done.2), channel_id=1, source_target_pairs={{0,1},{1,0},{2,3},{3,2},{4,5},{5,4},{6,7},{7,6},{8,9},{9,8},{10,11... | collective-permute-start | bytes 786440 | tf_op jit(solution)/shard_map/ppermute | solution.py:211
  69.0 3.0 %collective-permute-start.6 = (bf16[128,1024]{1,0:T(8,128)(2,1)S(1)}, bf16[128,1024]{1,0:T(8,128)(2,1)S(1)}, u32[]{:S(2)}, u32[]{:S(2)}) collective-permute-start(bf16[128,1024]{1,0:T(8,128)(2,1)S(1)} %collective-permute-done.5), channel_id=1, source_target_pairs={{0,1},{1,0},{2,3},{3,2},{4,5},{5,4},{6,7},{7,6},{8,9},{9,8},{10,11... | collective-permute-start | bytes 786440 | tf_op jit(solution)/shard_map/ppermute | solution.py:211
  94.7 7.2 %collective-permute-start.14 = (f32[8,2,128]{2,1,0:T(2,128)}, f32[8,2,128]{2,1,0:T(2,128)S(1)}, u32[]{:S(2)}, u32[]{:S(2)}) collective-permute-start(f32[8,2,128]{2,1,0:T(2,128)} %get-tuple-element.21), channel_id=1, source_target_pairs={{0,2},{1,3},{2,4},{3,5},{4,6},{5,7},{6,8},{7,9},{8,10},{9,11},{10,... | collective-permute-start | bytes 24584 | tf_op jit(solution)/shard_map/ppermute | solution.py:211
  99.9 8.4 %collective-permute-start.13 = (f32[8,2,128]{2,1,0:T(2,128)}, f32[8,2,128]{2,1,0:T(2,128)S(1)}, u32[]{:S(2)}, u32[]{:S(2)}) collective-permute-start(f32[8,2,128]{2,1,0:T(2,128)} %get-tuple-element.21), channel_id=1, source_target_pairs={{1,4},{3,6},{5,8},{7,10},{9,12},{11,14},{4,1},{6,3},{8,5},{10,7},{... | collective-permute-start | bytes 24584 | tf_op jit(solution)/shard_map/ppermute | solution.py:211
  100.6 6.0 %collective-permute-start.17 = (f32[8,2,128]{2,1,0:T(2,128)}, f32[8,2,128]{2,1,0:T(2,128)S(1)}, u32[]{:S(2)}, u32[]{:S(2)}) collective-permute-start(f32[8,2,128]{2,1,0:T(2,128)} %get-tuple-element.21), channel_id=1, source_target_pairs={{2,0},{3,1},{4,2},{5,3},{6,4},{7,5},{8,6},{9,7},{10,8},{11,9},{12,... | collective-permute-start | bytes 24584 | tf_op jit(solution)/shard_map/ppermute | solution.py:211
  101.9 6.4 %collective-permute-start.15 = (f32[8,2,128]{2,1,0:T(2,128)S(1)}, f32[8,2,128]{2,1,0:T(2,128)S(1)}, u32[]{:S(2)}, u32[]{:S(2)}) collective-permute-start(f32[8,2,128]{2,1,0:T(2,128)S(1)} %collective-permute-done.14), channel_id=1, source_target_pairs={{0,1},{1,0},{2,3},{3,2},{4,5},{5,4},{6,7},{7,6},{8,9},{9,8},{10,11... | collective-permute-start | bytes 24584 | tf_op jit(solution)/shard_map/ppermute | solution.py:211
  106.6 2.9 %collective-permute-start.16 = (f32[8,2,128]{2,1,0:T(2,128)}, f32[8,2,128]{2,1,0:T(2,128)S(1)}, u32[]{:S(2)}, u32[]{:S(2)}) collective-permute-start(f32[8,2,128]{2,1,0:T(2,128)} %get-tuple-element.21), channel_id=1, source_target_pairs={{0,1},{1,0},{2,3},{3,2},{4,5},{5,4},{6,7},{7,6},{8,9},{9,8},{10,11... | collective-permute-start | bytes 24584 | tf_op jit(solution)/shard_map/ppermute | solution.py:211
  106.6 4.8 %collective-permute-start.18 = (f32[8,2,128]{2,1,0:T(2,128)S(1)}, f32[8,2,128]{2,1,0:T(2,128)S(1)}, u32[]{:S(2)}, u32[]{:S(2)}) collective-permute-start(f32[8,2,128]{2,1,0:T(2,128)S(1)} %collective-permute-done.17), channel_id=1, source_target_pairs={{0,1},{1,0},{2,3},{3,2},{4,5},{5,4},{6,7},{7,6},{8,9},{9,8},{10,11... | collective-permute-start | bytes 24584 | tf_op jit(solution)/shard_map/ppermute | solution.py:211
  123.9 2.6 %copy-start.10 = (bf16[128,1024]{1,0:T(8,128)(2,1)S(1)}, bf16[128,1024]{1,0:T(8,128)(2,1)}, u32[]{:S(2)}) copy-start(bf16[128,1024]{1,0:T(8,128)(2,1)} %get-tuple-element.23) | copy-start | bytes 786436
  126.4 2.5 %copy-start.5 = (bf16[128,1024]{1,0:T(8,128)(2,1)S(1)}, bf16[128,1024]{1,0:T(8,128)(2,1)}, u32[]{:S(2)}) copy-start(bf16[128,1024]{1,0:T(8,128)(2,1)} %get-tuple-element.22) | copy-start | bytes 786436
  126.4 2.5 %copy-start.8 = (f32[128]{0:T(128)S(1)}, f32[128]{0:T(128)}, u32[]{:S(2)}) copy-start(f32[128]{0:T(128)} %copy-done.7) | copy-start | bytes 1540
  132.5 5.8 %copy-start.4 = (bf16[128,1024]{1,0:T(8,128)(2,1)S(1)}, bf16[128,1024]{1,0:T(8,128)(2,1)}, u32[]{:S(2)}) copy-start(bf16[128,1024]{1,0:T(8,128)(2,1)} %get-tuple-element.20) | copy-start | bytes 786436
  133.6 29.3 %all-to-all-start = ((bf16[128,16,160]{0,2,1:T(8,128)(2,1)}), bf16[128,16,160]{0,2,1:T(8,128)(2,1)S(1)}, u32[]{:S(2)}, u32[]{:S(2)}) async-start(bf16[128,16,160]{0,2,1:T(8,128)(2,1)} %bitcast.84), calls=%async_computation | async-start | bytes 1310720 | tf_op jit(solution)/shard_map/all_to_all | solution.py:310
Sparse Core Ops, SparseCore 0:
  132.7 58.9 all-gather.1

commit v2 on v1

v2 whole, which is shorter than its diff:
```python
import functools

import jax
import jax.numpy as jnp
from jax import lax
from jax.experimental import pallas as pl
from jax.experimental.pallas import tpu as pltpu
from jax.sharding import PartitionSpec as P

HEADS = 8
REACH = 3
HEAD_DIM = 128
norm_eps = 1e-05
neg_fill = -1e30
MEL_PITCH = 84
SCALE = HEAD_DIM ** (-0.5)


def dot_nt(a, b):
    return lax.dot_general(a, b, (((1,), (1,)), ((), ())), preferred_element_type=jnp.float32)


def dot_tn(a, b):
    return lax.dot_general(a, b, (((0,), (0,)), ((), ())), preferred_element_type=jnp.float32)


def dot_nn(a, b):
    return jnp.dot(a, b, preferred_element_type=jnp.float32)


MESH = pl.DeviceIdType.MESH


class Exchange:
    def __init__(self, size, x_ref, out_ref, send, recv):
        self.size, self.x, self.out, self.send, self.recv = size, x_ref, out_ref, send, recv
        self.me = lax.axis_index("tm")
        self.odd = lax.rem(self.me, 2)
        self.sibling = self.me + 1 - 2 * self.odd
        self.far = self.me - 3 + 6 * self.odd
        self.has_low = self.me >= 2
        self.has_high = self.me + 2 < size
        self.has_far = jnp.logical_and(self.far >= 0, self.far < size)

    def copy(self, src, slot, sem, target):
        return pltpu.make_async_remote_copy(
            src_ref=src,
            dst_ref=self.out.at[slot],
            send_sem=self.send.at[sem],
            recv_sem=self.recv.at[sem],
            device_id={"tm": target},
            device_id_type=MESH,
        )

    def up(self):
        return self.copy(self.x, 1, 0, self.me + 2)

    def down(self):
        return self.copy(self.x, 5, 1, self.me - 2)

    def across(self):
        return self.copy(self.x, 2 + 2 * self.odd, 2, self.sibling)

    def remote(self):
        return self.copy(self.x, 6 - 6 * self.odd, 3, self.far)

    def pass_low(self):
        return self.copy(self.out.at[1], 2 * self.odd, 4, self.sibling)

    def pass_high(self):
        return self.copy(self.out.at[5], 4 + 2 * self.odd, 5, self.sibling)

    def local(self):
        return pltpu.make_async_copy(self.x, self.out.at[3], self.send.at[6])

    def begin(self):
        barrier = pltpu.get_barrier_semaphore()

        def greet(target):
            pl.semaphore_signal(barrier, inc=1, device_id={"tm": target}, device_id_type=MESH)

        greet(self.sibling)
        pl.when(self.has_low)(lambda: greet(self.me - 2))
        pl.when(self.has_high)(lambda: greet(self.me + 2))
        pl.when(self.has_far)(lambda: greet(self.far))
        self.local().start()
        for slot in range(7):
            if slot != 3:
                other = self.me + slot - 3
                outside = jnp.logical_or(other < 0, other >= self.size)

                @pl.when(outside)
                def _(slot=slot):
                    self.out[slot] = jnp.zeros(self.out.shape[1:], self.out.dtype)

        peers = 1
        for has in (self.has_low, self.has_high, self.has_far):
            peers += jnp.where(has, 1, 0)
        pl.semaphore_wait(barrier, peers)
        pl.when(self.has_high)(lambda: self.up().start())
        pl.when(self.has_low)(lambda: self.down().start())
        pl.when(self.has_far)(lambda: self.remote().start())
        self.across().start()

    def forward(self):
        @pl.when(self.has_low)
        def _():
            self.up().wait_recv()
            self.pass_low().start()

        @pl.when(self.has_high)
        def _():
            self.down().wait_recv()
            self.pass_high().start()

    def finish(self):
        self.local().wait()
        self.across().wait()
        pl.when(self.has_far)(lambda: self.remote().wait())

        @pl.when(self.has_low)
        def _():
            self.down().wait_send()
            self.pass_low().wait()

        @pl.when(self.has_high)
        def _():
            self.up().wait_send()
            self.pass_high().wait()


EXCHANGE_SEMS = [pltpu.SemaphoreType.DMA((7,)), pltpu.SemaphoreType.DMA((6,))]


def exchange_kernel(size, x_ref, out_ref, send, recv):
    exchange = Exchange(size, x_ref, out_ref, send, recv)
    exchange.begin()
    exchange.forward()
    exchange.finish()


def gathered_window(x, size):
    out = pl.pallas_call(
        functools.partial(exchange_kernel, size),
        out_shape=jax.ShapeDtypeStruct((7,) + x.shape, x.dtype),
        in_specs=[pl.BlockSpec(memory_space=pltpu.VMEM)],
        out_specs=pl.BlockSpec(memory_space=pltpu.VMEM),
        scratch_shapes=EXCHANGE_SEMS,
        compiler_params=pltpu.CompilerParams(collective_id=1, has_side_effects=True),
        name="exchange",
    )(x)
    return out.reshape((7 * x.shape[0],) + x.shape[1:])


def subsample_kernel(
    size,
    x_ref,
    stem_ref,
    mid_dw_ref,
    mid_pw_ref,
    last_dw_ref,
    last_pw_ref,
    cot_ref,
    flat_ref,
    window_ref,
    even,
    odd,
    second,
    shifted,
    send,
    recv,
):
    exchange = Exchange(size, cot_ref, window_ref, send, recv)
    exchange.begin()
    rows = x_ref.shape[0] // 4
    main = rows - 8
    mids = second.shape[0] - 1
    span = shifted.shape[1] - 256
    odd[0] = jnp.zeros(odd.shape[1:], odd.dtype)
    second[0] = jnp.zeros(second.shape[1:], second.dtype)
    for i in range(4):
        shifted[i] = stem_ref[8 - 2 * i : 8 - 2 * i + span + 256, :]

    def step(k, half):
        def stem(i):
            start = pl.multiple_of(span - 8 * k, 8)
            taps = shifted[i, pl.ds(start, 256), :].astype(jnp.bfloat16)
            return jnp.maximum(dot_nn(x_ref[...], taps), 0.0).reshape(even.shape)

        m = 2 * k + half
        even[...] = stem(2 * half)
        odd[1 - half] = stem(2 * half + 1)
        parts = (odd.at[half], even, odd.at[1 - half])
        early = jnp.zeros((main, 256), jnp.float32)
        late = jnp.zeros((rows, 256), jnp.float32)
        for df in range(3):
            src = parts[df]
            for dt in range(3):
                tap = mid_dw_ref[3 * dt + df : 3 * dt + df + 1, :]
                phase = (3, 0, 1)[dt]
                start = 7 if dt == 0 else 8
                early += src[phase, start : start + main, :] * tap
                late += src[dt + 1] * tap
        weight = mid_pw_ref[...]
        second[m + 1, 0, 8:rows, :] = jnp.maximum(dot_nn(early.astype(jnp.bfloat16), weight), 0.0)
        second[m + 1, 1] = jnp.maximum(dot_nn(late.astype(jnp.bfloat16), weight), 0.0)

    def body(k, _):
        step(k, 0)
        step(k, 1)
        return 0

    lax.fori_loop(0, mids // 2, body, 0)
    exchange.forward()
    for f in range(mids // 2):
        total = jnp.zeros((main, 256), jnp.float32)
        for df in range(3):
            for dt in range(3):
                tap = last_dw_ref[3 * dt + df : 3 * dt + df + 1, :]
                phase = (1, 0, 1)[dt]
                start = 7 if dt == 0 else 8
                total += second[2 * f + df, phase, start : start + main, :] * tap
        out = jnp.maximum(dot_nn(total.astype(jnp.bfloat16), last_pw_ref[...]), 0.0)
        flat_ref[:, f * 256 : (f + 1) * 256] = out.astype(jnp.bfloat16)
    exchange.finish()


def subsample(
    size,
    features,
    halo,
    stem_kernel,
    mid_depthwise,
    mid_pointwise,
    last_depthwise,
    last_pointwise,
    cotangent,
):
    feat_rows, mel = features.shape
    main = feat_rows // 8
    rows = main + 8
    channels = stem_kernel.shape[-1]
    mids = mel // 4
    series = jnp.concatenate([jnp.zeros((56, mel), features.dtype), halo, features], axis=0)
    series = jnp.pad(series, ((0, 0), (1, MEL_PITCH - mel - 1)))
    late = jnp.pad(series, ((1, 0), (0, 0)))[:-1].reshape(rows, 8 * MEL_PITCH)
    tail = series.reshape(rows, 8 * MEL_PITCH)[:, 7 * MEL_PITCH :]
    wide = jnp.concatenate([late, tail], axis=1)
    x = jnp.concatenate(
        [wide[:, 2 * p * MEL_PITCH : (2 * p + 3) * MEL_PITCH] for p in range(4)], axis=0
    )
    x = jnp.pad(x, ((0, 0), (0, 256 - 3 * MEL_PITCH)))
    base = jnp.pad(stem_kernel.astype(jnp.float32), ((0, 0), (0, MEL_PITCH - 3), (0, 0)))
    base = base.reshape(3 * MEL_PITCH, channels)
    base = jnp.pad(base, ((mel + 8, 256 - 3 * MEL_PITCH), (0, 0)))
    return pl.pallas_call(
        functools.partial(subsample_kernel, size),
        out_shape=(
            jax.ShapeDtypeStruct((main, (mids // 2) * channels), jnp.bfloat16),
            jax.ShapeDtypeStruct((7,) + cotangent.shape, jnp.bfloat16),
        ),
        in_specs=[pl.BlockSpec(memory_space=pltpu.VMEM)] * 7,
        out_specs=(pl.BlockSpec(memory_space=pltpu.VMEM),) * 2,
        scratch_shapes=[
            pltpu.VMEM((4, rows, channels), jnp.float32),
            pltpu.VMEM((2, 4, rows, channels), jnp.float32),
            pltpu.VMEM((mids + 1, 2, rows, channels), jnp.float32),
            pltpu.VMEM((4, mel + 256, channels), jnp.float32),
        ]
        + EXCHANGE_SEMS,
        compiler_params=pltpu.CompilerParams(
            vmem_limit_bytes=40 * 1024 * 1024, collective_id=0, has_side_effects=True
        ),
        cost_estimate=pl.CostEstimate(
            flops=20_000_000_000, bytes_accessed=2_000_000, transcendentals=0
        ),
        name="subsample",
    )(
        x,
        base,
        mid_depthwise.reshape(9, channels).astype(jnp.float32),
        mid_pointwise,
        last_depthwise.reshape(9, channels).astype(jnp.float32),
        last_pointwise,
        cotangent,
    )


def segments(positions, bounds_ref):
    found = jnp.zeros(positions.shape, jnp.int32)
    for u in range(bounds_ref.shape[0]):
        inside = (positions >= bounds_ref[u, 0]) & (positions < bounds_ref[u, 1])
        found = jnp.where(inside, u + 1, found)
    return found


def attention_kernel(
    size,
    proj_ref,
    do_ref,
    bounds_ref,
    live_ref,
    out_ref,
    grad_ref,
    bias_ref,
    bias2_ref,
    stat_ref,
    send,
    recv,
):
    rows = out_ref.shape[0]
    window = proj_ref.shape[0]
    width = out_ref.shape[1]
    own = slice(REACH * rows, (REACH + 1) * rows)
    me = lax.axis_index("tm")
    barrier = pltpu.get_barrier_semaphore()
    offsets = [o for o in range(-REACH, REACH + 1) if o]

    def when_there(offset, action):
        other = me + offset
        pl.when(jnp.logical_and(other >= 0, other < size))(lambda: action(offset))

    def greet(offset):
        pl.semaphore_signal(barrier, inc=1, device_id={"tm": me + offset}, device_id_type=MESH)

    def copy(offset):
        slot = REACH + offset
        return pltpu.make_async_remote_copy(
            src_ref=stat_ref.at[REACH],
            dst_ref=stat_ref.at[REACH - offset],
            send_sem=send.at[slot],
            recv_sem=recv.at[2 * REACH - slot],
            device_id={"tm": me + offset},
            device_id_type=MESH,
        )

    def incoming(offset):
        slot = REACH + offset
        return pltpu.make_async_remote_copy(
            src_ref=stat_ref.at[REACH],
            dst_ref=stat_ref.at[slot],
            send_sem=send.at[slot],
            recv_sem=recv.at[slot],
            device_id={"tm": me + offset},
            device_id_type=MESH,
        )

    for offset in offsets:
        when_there(offset, greet)

        @pl.when(jnp.logical_or(me + offset < 0, me + offset >= size))
        def _(offset=offset):
            stat_ref[REACH + offset] = jnp.zeros(stat_ref.shape[1:], jnp.float32)

    first = (me - REACH) * rows
    own_col = segments(me * rows + lax.broadcasted_iota(jnp.int32, (rows, 128), 0), bounds_ref)
    own_row = segments(me * rows + lax.broadcasted_iota(jnp.int32, (8, rows), 1), bounds_ref)[0:1]
    for b in range(2 * REACH + 1):
        place = first + b * rows
        live = live_ref[0, b] == 1
        col = segments(place + lax.broadcasted_iota(jnp.int32, (rows, 128), 0), bounds_ref)
        row = segments(place + lax.broadcasted_iota(jnp.int32, (8, rows), 1), bounds_ref)[0:1]
        span = slice(b * rows, (b + 1) * rows)
        bias_ref[span, :] = jnp.where((col[:, 0:1] == own_row) & live, 0.0, neg_fill)
        bias2_ref[:, span] = jnp.where((own_col[:, 0:1] == row) & live, 0.0, neg_fill)

    def column(group, h):
        return pl.ds(pl.multiple_of(group * width + h * HEAD_DIM, HEAD_DIM), HEAD_DIM)

    def forward(h):
        scores = dot_nt(proj_ref[:, column(1, h)], proj_ref[own, column(0, h)]) * SCALE
        scores = scores + bias_ref[...]
        top = jnp.max(scores, axis=0, keepdims=True)
        weights = jnp.exp(scores - top)
        total = jnp.sum(weights, axis=0, keepdims=True)
        probs = (weights * (1.0 / total)).astype(jnp.bfloat16)
        out = dot_tn(probs, proj_ref[:, column(2, h)])
        out_ref[:, column(0, h)] = out.astype(jnp.bfloat16)
        prod = do_ref[own, column(0, h)].astype(jnp.float32) * out
        stat_ref[REACH, h, 0:1, :] = top + jnp.log(total)
        stat_ref[REACH, h, 1:2, :] = jnp.sum(prod.T, axis=0, keepdims=True)

    def query_pass(h):
        keys = proj_ref[:, column(1, h)]
        scores = dot_nt(keys, proj_ref[own, column(0, h)]) * SCALE
        weights = jnp.exp(scores + bias_ref[...] - stat_ref[REACH, h, 0:1, :])
        dprob = dot_nt(proj_ref[:, column(2, h)], do_ref[own, column(0, h)])
        dscore = (weights * (dprob - stat_ref[REACH, h, 1:2, :])).astype(jnp.bfloat16)
        grad_ref[:, column(0, h)] = (dot_tn(dscore, keys) * SCALE).astype(jnp.bfloat16)

    def key_pass(h):
        queries = proj_ref[:, column(0, h)]
        douts = do_ref[:, column(0, h)]
        blocks = range(2 * REACH + 1)
        log_norms = jnp.concatenate([stat_ref[b, h, 0:1, :] for b in blocks], axis=1)
        deltas = jnp.concatenate([stat_ref[b, h, 1:2, :] for b in blocks], axis=1)
        scores = dot_nt(proj_ref[own, column(1, h)], queries) * SCALE
        weights = jnp.exp(scores + bias2_ref[...] - log_norms)
        dprob = dot_nt(proj_ref[own, column(2, h)], douts)
        dscore = (weights * (dprob - deltas)).astype(jnp.bfloat16)
        grad_ref[:, column(1, h)] = (dot_nn(dscore, queries) * SCALE).astype(jnp.bfloat16)
        grad_ref[:, column(2, h)] = dot_nn(weights.astype(jnp.bfloat16), douts).astype(jnp.bfloat16)

    def over_heads(work):
        def pair(i, _):
            work(2 * i)
            work(2 * i + 1)
            return 0

        lax.fori_loop(0, HEADS // 2, pair, 0)

    over_heads(forward)
    peers = 0
    for offset in offsets:
        peers += jnp.where(jnp.logical_and(me + offset >= 0, me + offset < size), 1, 0)
    pl.semaphore_wait(barrier, peers)
    for offset in offsets:
        when_there(offset, lambda o: copy(o).start())
    over_heads(query_pass)
    for offset in offsets:
        when_there(offset, lambda o: incoming(o).wait_recv())
    over_heads(key_pass)
    for offset in offsets:
        when_there(offset, lambda o: copy(o).wait_send())


def attention(size, projected, d_attention, utt_bounds, live_blocks):
    window = projected.shape[0]
    rows = window // (2 * REACH + 1)
    width = d_attention.shape[1]
    vmem = pl.BlockSpec(memory_space=pltpu.VMEM)
    smem = pl.BlockSpec(memory_space=pltpu.SMEM)
    return pl.pallas_call(
        functools.partial(attention_kernel, size),
        out_shape=(
            jax.ShapeDtypeStruct((rows, width), jnp.bfloat16),
            jax.ShapeDtypeStruct((rows, 3 * width), jnp.bfloat16),
        ),
        in_specs=[vmem, vmem, smem, smem],
        out_specs=(vmem, vmem),
        scratch_shapes=[
            pltpu.VMEM((window, rows), jnp.float32),
            pltpu.VMEM((rows, window), jnp.float32),
            pltpu.VMEM((2 * REACH + 1, HEADS, 2, rows), jnp.float32),
            pltpu.SemaphoreType.DMA((2 * REACH + 1,)),
            pltpu.SemaphoreType.DMA((2 * REACH + 1,)),
        ],
        compiler_params=pltpu.CompilerParams(
            vmem_limit_bytes=32 * 1024 * 1024, collective_id=2, has_side_effects=True
        ),
        cost_estimate=pl.CostEstimate(
            flops=20_000_000_000, bytes_accessed=8_000_000, transcendentals=2_000_000
        ),
        name="attention",
    )(projected, d_attention, utt_bounds, live_blocks)


def per_device(
    size,
    features,
    stem_kernel,
    mid_depthwise,
    mid_pointwise,
    last_depthwise,
    last_pointwise,
    proj_weight,
    norm_gain,
    qkv_weight,
    out_weight,
    cotangent,
    utt_bounds,
    live_blocks,
):
    halo = lax.ppermute(features[-8:], "tm", [(i, i + 1) for i in range(size - 1)])
    flat_rows, cot_window = subsample(
        size,
        features,
        halo,
        stem_kernel,
        mid_depthwise,
        mid_pointwise,
        last_depthwise,
        last_pointwise,
        cotangent,
    )
    cot_window = cot_window.reshape(-1, cotangent.shape[1])

    frames = dot_nn(flat_rows, proj_weight).astype(jnp.bfloat16)
    frames_f = frames.astype(jnp.float32)
    row_mean = jnp.mean(frames_f, axis=-1, keepdims=True)
    centered = frames_f - row_mean
    inv_std = lax.rsqrt(jnp.mean(centered * centered, axis=-1, keepdims=True) + norm_eps)
    normalized = centered * inv_std
    normed = (normalized * norm_gain).astype(jnp.bfloat16)
    normed_window = gathered_window(normed, size)
    normed_window, flat_sent, cot_window = lax.optimization_barrier(
        (normed_window, flat_rows, cot_window)
    )
    own_cols = size * (flat_rows.shape[1] // size)
    columns = lax.all_to_all(flat_sent[:, :own_cols], "tm", 1, 0, tiled=True)
    d_attention = dot_nt(cot_window, out_weight).astype(jnp.bfloat16)
    projected = dot_nn(normed_window, qkv_weight).astype(jnp.bfloat16)
    mixed, grads = attention(size, projected, d_attention, utt_bounds, live_blocks)
    grads, columns = lax.optimization_barrier((grads, columns))
    block_out = (frames_f + dot_nn(mixed, out_weight)).astype(jnp.bfloat16)
    grad_normed = dot_nt(grads, qkv_weight)
    scaled_grad = grad_normed * norm_gain
    ln_grad = inv_std * (
        scaled_grad
        - jnp.mean(scaled_grad, axis=-1, keepdims=True)
        - normalized * jnp.mean(scaled_grad * normalized, axis=-1, keepdims=True)
    )
    frame_grads = (cotangent.astype(jnp.float32) + ln_grad).astype(jnp.bfloat16)
    all_grads = lax.all_gather(frame_grads, "tm", axis=0, tiled=True)
    proj_grads = dot_tn(columns, all_grads)
    return (block_out, frame_grads, proj_grads)


def solution(mesh):
    split = P(("groups", "tm"), None)
    in_specs = (split,) + (P(),) * 9 + (split, P("groups", None), split)
    return jax.shard_map(
        functools.partial(per_device, mesh.shape["tm"]),
        mesh=mesh,
        in_specs=in_specs,
        out_specs=(split, split, split),
        check_vma=False,
    )
```

time: 204 us -> 167 us (0.82)
  starting transfers between devices: 42.5 us -> 11.1 us
  Pallas kernels: 32.4 us -> 45.2 us
  other arithmetic: 14.1 us -> 3.03 us
  waiting for transfers between devices: 55.9 us -> 49.6 us
    ppermute x18 -> x0, starting transfers between devices: 35.8 us -> none  [moved(): return lax.ppermute(value, 'tm', pairs)]
    all_to_all x1, waiting for transfers between devices: 23.4 us -> 0.01 us  [per_device(): columns = lax.all_to_all(flat_sent[:, :own_cols], 'tm', 1, 0, tiled=True)]
    all_gather x1, waiting for transfers between devices: 28.8 us -> 49.6 us  [per_device(): all_grads = lax.all_gather(frame_grads, 'tm', axis=0, tiled=True)]
    pallas_call x3, Pallas kernels: 32.4 us -> 45.2 us  [the longest x1 16.9 us: gathered_window(): pl.pallas_call(functools.partial(exchange_kernel, size), out_shape=jax.Sh...]
    gather x1 -> x0, other arithmetic: 4.58 us -> none  [per_device(): flag = jnp.repeat(live_blocks[0], rows, total_repeat_length=window)]
    dot_general x3, matrix products: 9.82 us -> 14.3 us  [dot_nn(): return jnp.dot(a, b, preferred_element_type=jnp.float32)]
    unnamed x12 -> x0, other arithmetic: 4.35 us -> none
    all_to_all x1, starting transfers between devices: 4.73 us -> 8.76 us  [per_device(): columns = lax.all_to_all(flat_sent[:, :own_cols], 'tm', 1, 0, tiled=True)]
  transfers between devices with their start and end apart: 21 -> 3, of which waited for: 4 -> 1; matrix products, arithmetic and copies ran while one was open for 14% -> 10% of each run, Pallas kernels for 6% -> 8%
where the time goes in v2:
time: 167 us; the launch traced here: 166 us
  waiting for transfers between devices  49.6 us (30%)
  Pallas kernels  45.2 us (27%)
  matrix products  25.5 us (15%)
  local copies, waits for them, and re-layouts  17.5 us (10%)
  between operations  14.3 us (9%)
  starting transfers between devices  11.1 us (7%)
  other arithmetic  3.03 us (2%)
    all_gather x1, waiting for transfers between devices, per_device(): all_grads = lax.all_gather(frame_grads, 'tm', axis=0, tiled=True)  49.6 us
    pallas_call x1, Pallas kernels, gathered_window(): pl.pallas_call(functools.partial(exchange_kernel, size), out_shape=jax.Sh...  16.9 us
    pallas_call x1, Pallas kernels, subsample(): pl.pallas_call(functools.partial(subsample_kernel, size), out_shape=(jax....  15.6 us
    dot_general x3, matrix products, dot_nn(): return jnp.dot(a, b, preferred_element_type=jnp.float32)  14.3 us
    pallas_call x1, Pallas kernels, attention(): pl.pallas_call(functools.partial(attention_kernel, size), out_shape=(jax....  12.6 us
    all_to_all x1, starting transfers between devices, per_device(): columns = lax.all_to_all(flat_sent[:, :own_cols], 'tm', 1, 0, tiled=True)  8.76 us
    dot_general x2, matrix products, dot_nt(): lax.dot_general(a, b, (((1,), (1,)), ((), ())), preferred_element_type=jn...  7.32 us
    dot_general x1, matrix products, dot_tn(): lax.dot_general(a, b, (((0,), (0,)), ((), ())), preferred_element_type=jn...  3.9 us
  transfers between devices with their start and end apart: 3, of which 1 were waited for; matrix products, arithmetic and copies ran while one was open for 10% of the time, Pallas kernels for 8%

profile of v2, /device:TPU:0, one launch (start us, length us, event | category | flops | bytes accessed | tf_op | source)
XLA Modules:
  0.0 166.3 jit_solution(7374824997163725214)
XLA Ops:
  7.2 0.0 copy-start
  7.2 0.0 copy-start.2
  7.2 0.0 copy-start.1
  7.2 1.0 slice.21
  8.2 2.3 %collective-permute-start = (bf16[8,80]{0,1:T(8,128)(2,1)S(1)}, bf16[8,80]{0,1:T(8,128)(2,1)S(1)}, u32[]{:S(2)}, u32[]{:S(2)}) collective-permute-start(bf16[8,80]{0,1:T(8,128)(2,1)S(1)} %slice.21), channel_id=1, source_target_pairs={{0,1},{1,2},{2,3},{3,4},{4,5},{5,6},{6,7},{7,8},{8,9},{9,10},{10,1... | collective-permute-start | bytes 3848 | tf_op jit(solution)/shard_map/ppermute | solution.py:474
  10.5 0.7 pad.26
  11.3 0.7 reshape.57.mid_dw_ref
  12.0 0.7 reshape.58.last_dw_ref
  12.7 0.8 copy.21.bounds_ref
  13.4 0.0 collective-permute-done
  13.5 1.1 concatenate.9
  14.6 0.1 pad.23
  14.6 0.8 pad_slice_fusion
  15.4 0.2 copy.20
  15.6 1.8 %copy.19 = bf16[1088,84]{1,0:T(8,128)(2,1)} copy(bf16[1088,84]{0,1:T(8,128)(2,1)} %pad_slice_fusion) | data formatting | bytes 365568 | tf_op jit(solution)/shard_map/slice | solution.py:246
  17.5 1.2 reshape.52
  18.7 0.7 fusion.12
  19.4 0.9 reshape.53
  20.3 1.0 slice.31
  21.3 1.0 fusion.9.x_ref
  22.3 0.0 copy-done.2
  22.3 0.0 copy-done.1
  22.3 0.0 copy-start.3
  22.3 0.9 copy-done.3
  23.2 15.6 %subsample.1 = (bf16[128,2560]{1,0:T(8,128)(2,1)S(1)}, bf16[7,128,1024]{2,1,0:T(8,128)(2,1)S(1)}) custom-call(bf16[544,256]{1,0:T(8,128)(2,1)S(1)} %fusion.9.x_ref, f32[344,256]{1,0:T(8,128)S(1)} %pad_convert_fusion.stem_ref, f32[9,256]{1,0:T(8,128)S(1)} %reshape.57.mid_dw_ref, bf16[256,256]{1,0:T(8,128)(2,1)S(1)} %copy-done.2, ...), custom_call_target="tpu_custom_call" | custom-call | flops 20000000000 | bytes 2000000 | tf_op jit(solution)/shard_map/subsample/pallas_call | solution.py:256
  38.8 0.0 copy-start.5
  38.8 1.2 copy-done.5
  40.1 0.0 copy-start.10
  40.1 3.5 %fusion.13 = (f32[128]{0:T(128)S(1)}, f32[128,1024]{1,0:T(8,128)S(1)}) fusion(bf16[128,2560]{1,0:T(8,128)(2,1)S(1)} %get-tuple-element.18, bf16[2560,1024]{1,0:T(8,128)(2,1)} %param.19), kind=kOutput, calls=%fused_computation.31 | convolution fusion | flops 671481728 | bytes 6423040 | tf_op jit(solution)/shard_map/dot_general | solution.py:28
  43.6 0.0 copy-start.7
  43.6 0.2 multiply_reduce_fusion.1
  43.8 0.6 copy-done.7
  44.4 0.0 copy-done.10
  44.4 0.8 multiply_convert_fusion.x_ref
  45.2 16.9 %exchange.1 = bf16[7,128,1024]{2,1,0:T(8,128)(2,1)} custom-call(bf16[128,1024]{1,0:T(8,128)(2,1)} %multiply_convert_fusion.x_ref), custom_call_target="tpu_custom_call" | custom-call | tf_op jit(solution)/shard_map/exchange/pallas_call | solution.py:143
  62.2 1.1 copy.22
  63.2 8.8 %all-to-all-start = ((bf16[128,16,160]{0,2,1:T(8,128)(2,1)}), bf16[128,16,160]{0,2,1:T(8,128)(2,1)}, u32[]{:S(2)}, u32[]{:S(2)}) async-start(bf16[128,16,160]{0,2,1:T(8,128)(2,1)} %bitcast.22), calls=%async_computation | async-start | bytes 1310720 | tf_op jit(solution)/shard_map/all_to_all | solution.py:500
  72.0 0.0 all-gather.2.cloned.1.call-start
  72.1 0.0 copy-start.6
  72.1 8.6 %convolution_convert_fusion.proj_ref = bf16[896,3072]{1,0:T(8,128)(2,1)S(1)} fusion(bf16[896,1024]{1,0:T(8,128)(2,1)} %bitcast.23, bf16[1024,3072]{1,0:T(8,128)(2,1)} %param.21), kind=kOutput, calls=%fused_computation | convolution fusion | flops 5639897088 | bytes 13631488 | tf_op jit(solution)/shard_map/dot_general | solution.py:28
  80.7 0.0 copy-done
  80.7 0.0 copy-done.6
  80.7 0.0 copy-start.4
  80.7 2.1 %convolution_convert_fusion.1.do_ref = bf16[896,1024]{1,0:T(8,128)(2,1)S(1)} fusion(bf16[896,1024]{1,0:T(8,128)(2,1)S(1)} %bitcast.21, bf16[1024,1024]{1,0:T(8,128)(2,1)S(1)} %copy-done), kind=kOutput, calls=%fused_computation.1 | convolution fusion | flops 1879965696 | bytes 5767168 | tf_op jit(solution)/shard_map/dot_general | solution.py:20
  82.8 0.0 copy-done.4
  82.8 12.6 %attention.1 = (bf16[128,1024]{1,0:T(8,128)(2,1)S(1)}, bf16[128,3072]{1,0:T(8,128)(2,1)S(1)}) custom-call(bf16[896,3072]{1,0:T(8,128)(2,1)S(1)} %convolution_convert_fusion.proj_ref, bf16[896,1024]{1,0:T(8,128)(2,1)S(1)} %convolution_convert_fusion.1.do_ref, s32[8,2]{1,0:T(8,128)S(1)} %copy.21.bounds_ref, s32[1,7]{1,0:T(1,128)S(1)} %copy-done.4), custom_call_target="tpu_custom_call" | custom-call | flops 20000000000 | bytes 8000000 | tf_op jit(solution)/shard_map/attention/pallas_call | solution.py:433
  95.5 0.0 all-to-all-done
  95.5 2.0 %copy_bitcast_fusion = bf16[2048,160]{0,1:T(8,128)(2,1)} fusion(bf16[128,16,160]{0,2,1:T(8,128)(2,1)} %all-to-all-done), kind=kLoop, calls=%fused_computation.7 | loop fusion | bytes 1310720 | tf_op jit(solution)/shard_map/all_to_all | solution.py:500
  97.5 0.0 copy-start.8
  97.5 5.2 %fusion.11 = (f32[128]{0:T(128)S(1)}, f32[128]{0:T(128)S(1)}, f32[128,1024]{1,0:T(8,128)S(1)}) fusion(f32[128]{0:T(128)S(1)} %add_rsqrt_fusion, f32[128,1024]{1,0:T(8,128)} %copy-done.7, f32[128]{0:T(128)S(1)} %broadcast_multiply_fusion.2, f32[1024]{0:T(1024)S(1)} %copy-done.10, bf16[128,3072]{1,0:T(8,128)(2,1)S(1)} %get-tuple-element.19, ...), kind=kOutput, calls=%fused_computation.29 | convolution fusion | flops 806092544 | bytes 8132608 | tf_op jit(solution)/shard_map/dot_general | solution.py:20
  102.7 0.0 copy-start.9
  102.8 0.0 copy-done.8
  102.8 1.0 add_convert_fusion
  103.7 0.0 all-gather.2.cloned.1.call-update
  103.8 2.2 %fusion.1 = bf16[128,1024]{1,0:T(8,128)(2,1)} fusion(f32[128,1024]{1,0:T(8,128)} %copy-done.7, bf16[128,1024]{1,0:T(8,128)(2,1)S(1)} %get-tuple-element.16, bf16[1024,1024]{1,0:T(8,128)(2,1)S(1)} %copy-done), kind=kOutput, calls=%fused_computation.6 | convolution fusion | flops 268697600 | bytes 3145728 | tf_op jit(solution)/shard_map/dot_general | solution.py:28
  106.0 49.6 %all-gather.2.cloned.1.call-done = bf16[2048,1024]{1,0:T(8,128)(2,1)} async-done(((bf16[128,1024]{1,0:T(8,128)(2,1)}), bf16[2048,1024]{1,0:T(8,128)(2,1)}) %all-gather.2.cloned.1.call-update) | async-done | bytes 4194320 | tf_op jit(solution)/shard_map/all_gather | solution.py:514
  155.5 0.0 copy-done.9
  155.5 3.9 %fusion.14 = f32[160,1024]{1,0:T(8,128)} fusion(bf16[2048,160]{0,1:T(8,128)(2,1)S(1)} %copy-done.9, bf16[2048,1024]{1,0:T(8,128)(2,1)} %all-gather.2.cloned.1.call-done), kind=kOutput, calls=%fused_computation.32 | convolution fusion | flops 671088640 | bytes 5505024 | tf_op jit(solution)/shard_map/dot_general | solution.py:24
  (6 shorter events, 0.1 us)
Async XLA Ops:
  7.2 73.5 %copy-start = (bf16[1024,1024]{1,0:T(8,128)(2,1)S(1)}, bf16[1024,1024]{1,0:T(8,128)(2,1)}, u32[]{:S(2)}) copy-start(bf16[1024,1024]{1,0:T(8,128)(2,1)} %param.22) | copy-start | bytes 6291460
  7.2 15.1 %copy-start.2 = (bf16[256,256]{1,0:T(8,128)(2,1)S(1)}, bf16[256,256]{1,0:T(8,128)(2,1)}, u32[]{:S(2)}) copy-start(bf16[256,256]{1,0:T(8,128)(2,1)} %mid_pw_ref.1) | copy-start | bytes 393220
  7.2 15.1 %copy-start.1 = (bf16[128,1024]{1,0:T(8,128)(2,1)S(1)}, bf16[128,1024]{1,0:T(8,128)(2,1)}, u32[]{:S(2)}) copy-start(bf16[128,1024]{1,0:T(8,128)(2,1)} %cot_ref.1) | copy-start | bytes 786436
  8.2 5.3 %collective-permute-start = (bf16[8,80]{0,1:T(8,128)(2,1)S(1)}, bf16[8,80]{0,1:T(8,128)(2,1)S(1)}, u32[]{:S(2)}, u32[]{:S(2)}) collective-permute-start(bf16[8,80]{0,1:T(8,128)(2,1)S(1)} %slice.21), channel_id=1, source_target_pairs={{0,1},{1,2},{2,3},{3,4},{4,5},{5,6},{6,7},{7,8},{8,9},{9,10},{10,1... | collective-permute-start | bytes 3848 | tf_op jit(solution)/shard_map/ppermute | solution.py:474
  22.3 0.9 copy-start.3
  38.8 1.3 copy-start.5
  40.1 4.3 %copy-start.10 = (f32[1024]{0:T(1024)S(1)}, f32[1024]{0:T(1024)}, u32[]{:S(2)}) copy-start(f32[1024]{0:T(1024)} %param.20) | copy-start | bytes 12292
  43.6 0.8 copy-start.7
  63.2 32.3 %all-to-all-start = ((bf16[128,16,160]{0,2,1:T(8,128)(2,1)}), bf16[128,16,160]{0,2,1:T(8,128)(2,1)}, u32[]{:S(2)}, u32[]{:S(2)}) async-start(bf16[128,16,160]{0,2,1:T(8,128)(2,1)} %bitcast.22), calls=%async_computation | async-start | bytes 1310720 | tf_op jit(solution)/shard_map/all_to_all | solution.py:500
  72.0 83.5 %all-gather.2.cloned.1.call-start = ((), (), s32[]{:S(2)}) async-start(), calls=%async_computation.1 | async-start | bytes 4456448 | tf_op jit(solution)/shard_map/all_gather | solution.py:514
  72.1 8.7 %copy-start.6 = (bf16[7,128,1024]{2,1,0:T(8,128)(2,1)S(1)}, bf16[7,128,1024]{2,1,0:T(8,128)(2,1)}, u32[]{:S(2)}) copy-start(bf16[7,128,1024]{2,1,0:T(8,128)(2,1)} %copy-done.5) | copy-start | bytes 5505028
  80.7 2.1 %copy-start.4 = (s32[1,7]{1,0:T(1,128)S(1)}, s32[1,7]{1,0:T(1,128)}, u32[]{:S(2)}) copy-start(s32[1,7]{1,0:T(1,128)} %live_ref.1) | copy-start | bytes 88
  97.5 5.2 %copy-start.8 = (f32[128,1024]{1,0:T(8,128)S(1)}, f32[128,1024]{1,0:T(8,128)}, u32[]{:S(2)}) copy-start(f32[128,1024]{1,0:T(8,128)} %copy-done.7) | copy-start | bytes 1572868
  102.7 52.8 %copy-start.9 = (bf16[2048,160]{0,1:T(8,128)(2,1)S(1)}, bf16[2048,160]{0,1:T(8,128)(2,1)}, u32[]{:S(2)}) copy-start(bf16[2048,160]{0,1:T(8,128)(2,1)} %copy_bitcast_fusion) | copy-start | bytes 1966084
Sparse Core Ops, SparseCore 0:
  103.9 51.6 all-gather.1

commit v3 on v2

--- a/solution.py
+++ b/solution.py
@@ -150,6 +150,109 @@
         name="exchange",
     )(x)
     return out.reshape((7 * x.shape[0],) + x.shape[1:])
+
+
+def gather_kernel(size, x_ref, out_ref, send, recv, side_send, side_recv, own_sem):
+    chips = size // 2
+    half = chips // 2
+    rows = x_ref.shape[0]
+    piece = rows // 2
+    me = lax.axis_index("tm")
+    core = lax.rem(me, 2)
+    chip = me // 2
+    sibling = me + 1 - 2 * core
+    odd = lax.rem(chip, 2)
+    place = jnp.where(odd == 0, chip // 2, chips - 1 - chip // 2)
+
+    def device(offset):
+        spot = lax.rem(place + offset + 2 * chips, chips)
+        return jnp.where(spot < half, 2 * spot, 2 * (chips - 1 - spot) + 1) * 2 + core
+
+    def remote(src, dst, send_sem, recv_sem, target):
+        return pltpu.make_async_remote_copy(
+            src_ref=src,
+            dst_ref=dst,
+            send_sem=send_sem,
+            recv_sem=recv_sem,
+            device_id={"tm": target},
+            device_id_type=MESH,
+        )
+
+    def part(slot, c):
+        return out_ref.at[slot, pl.ds(c * piece, piece), :]
+
+    def along(way, k, c):
+        sign = 1 - 2 * way
+        slot = device(-sign * (k - 1))
+        src = x_ref.at[pl.ds(c * piece, piece), :] if k == 1 else part(slot, c)
+        index = (way, k - 1, c)
+        return remote(src, part(slot, c), send.at[index], recv.at[index], device(sign))
+
+    def arrived(way, k, c):
+        sign = 1 - 2 * way
+        slot = device(-sign * k)
+        index = (way, k - 1, c)
+        return remote(part(slot, c), part(slot, c), send.at[index], recv.at[index], device(sign))
+
+    def side(way, k, c):
+        slot = device(-(1 - 2 * way) * k)
+        index = (way, k - 1, c)
+        return remote(part(slot, c), part(slot, c), side_send.at[index], side_recv.at[index], sibling)
+
+    def side_arrived(way, k, c):
+        slot = device(-(1 - 2 * way) * k) + 1 - 2 * core
+        index = (way, k - 1, c)
+        return remote(part(slot, c), part(slot, c), side_send.at[index], side_recv.at[index], sibling)
+
+    def used(way, k, c):
+        return k < half or (k == half and c == way)
+
+    steps = [
+        (way, k, c)
+        for k in range(1, half + 1)
+        for c in range(2)
+        for way in range(2)
+        if used(way, k, c)
+    ]
+    barrier = pltpu.get_barrier_semaphore()
+    for target in (device(1), device(-1), sibling):
+        pl.semaphore_signal(barrier, inc=1, device_id={"tm": target}, device_id_type=MESH)
+    own = pltpu.make_async_copy(x_ref, out_ref.at[me], own_sem.at[0])
+    across = remote(x_ref, out_ref.at[me], own_sem.at[1], own_sem.at[2], sibling)
+    own.start()
+    pl.semaphore_wait(barrier, 3)
+    for c in range(2):
+        for way in range(2):
+            along(way, 1, c).start()
+    across.start()
+    for way, k, c in steps:
+        arrived(way, k, c).wait_recv()
+        if used(way, k + 1, c):
+            along(way, k + 1, c).start()
+        side(way, k, c).start()
+    own.wait()
+    across.wait()
+    for way, k, c in steps:
+        side_arrived(way, k, c).wait_recv()
+        side(way, k, c).wait_send()
+        along(way, k, c).wait_send()
+
+
+def gathered(x, size):
+    half = size // 4
+    out = pl.pallas_call(
+        functools.partial(gather_kernel, size),
+        out_shape=jax.ShapeDtypeStruct((size,) + x.shape, x.dtype),
+        in_specs=[pl.BlockSpec(memory_space=pltpu.VMEM)],
+        out_specs=pl.BlockSpec(memory_space=pltpu.VMEM),
+        scratch_shapes=[pltpu.SemaphoreType.DMA((2, half, 2))] * 4
+        + [pltpu.SemaphoreType.DMA((3,))],
+        compiler_params=pltpu.CompilerParams(
+            vmem_limit_bytes=32 * 1024 * 1024, collective_id=3, has_side_effects=True
+        ),
+        name="all_gather",
+    )(x)
+    return out.reshape((size * x.shape[0],) + x.shape[1:])
 
 
 def subsample_kernel(
@@ -511,7 +614,7 @@
         - normalized * jnp.mean(scaled_grad * normalized, axis=-1, keepdims=True)
     )
     frame_grads = (cotangent.astype(jnp.float32) + ln_grad).astype(jnp.bfloat16)
-    all_grads = lax.all_gather(frame_grads, "tm", axis=0, tiled=True)
+    all_grads = gathered(frame_grads, size)
     proj_grads = dot_tn(columns, all_grads)
     return (block_out, frame_grads, proj_grads)
 

time: 167 us -> 126 us (0.75)
  waiting for transfers between devices: 49.6 us -> 0.01 us
  Pallas kernels: 45.2 us -> 72.4 us
  between operations: 14.3 us -> 0.92 us
  matrix products: 25.5 us -> 22.3 us
    all_gather x1 -> x0, waiting for transfers between devices: 49.6 us -> none  [per_device(): all_grads = lax.all_gather(frame_grads, 'tm', axis=0, tiled=True)]
    pallas_call x0 -> x1, Pallas kernels: none -> 27.2 us  [gathered(): pl.pallas_call(functools.partial(gather_kernel, size), out_shape=jax.Shap...]
    dot_general x1, matrix products: 3.9 us -> 1.69 us  [dot_tn(): lax.dot_general(a, b, (((0,), (0,)), ((), ())), preferred_element_type=jn...]
    unnamed x23 -> x25, local copies, waits for them, and re-layouts: 3.52 us -> 3.52 us
  transfers between devices with their start and end apart: 3 -> 2, of which waited for: 1 -> 0; matrix products, arithmetic and copies ran while one was open for 10% -> 12% of each run, Pallas kernels for 8% -> 10%
where the time goes in v3:
time: 126 us
  Pallas kernels  72.4 us (57%)
  matrix products  22.3 us (18%)
  local copies, waits for them, and re-layouts  16.6 us (13%)
  starting transfers between devices  11.1 us (9%)
  other arithmetic  2.32 us (2%)
    pallas_call x1, Pallas kernels, gathered(): pl.pallas_call(functools.partial(gather_kernel, size), out_shape=jax.Shap...  27.2 us
    pallas_call x1, Pallas kernels, gathered_window(): pl.pallas_call(functools.partial(exchange_kernel, size), out_shape=jax.Sh...  16.9 us
    pallas_call x1, Pallas kernels, subsample(): pl.pallas_call(functools.partial(subsample_kernel, size), out_shape=(jax....  15.6 us
    dot_general x3, matrix products, dot_nn(): return jnp.dot(a, b, preferred_element_type=jnp.float32)  13.3 us
    pallas_call x1, Pallas kernels, attention(): pl.pallas_call(functools.partial(attention_kernel, size), out_shape=(jax....  12.7 us
    all_to_all x1, starting transfers between devices, per_device(): columns = lax.all_to_all(flat_sent[:, :own_cols], 'tm', 1, 0, tiled=True)  8.76 us
    dot_general x2, matrix products, dot_nt(): lax.dot_general(a, b, (((1,), (1,)), ((), ())), preferred_element_type=jn...  7.32 us
    unnamed x25, local copies, waits for them, and re-layouts  3.52 us
  transfers between devices with their start and end apart: 2, of which 0 were waited for; matrix products, arithmetic and copies ran while one was open for 12% of the time, Pallas kernels for 10%

profile of v3, /device:TPU:0, one launch (start us, length us, event | category | flops | bytes accessed | tf_op | source)
XLA Modules:
  0.0 125.6 jit_solution(11483339417793430165)
XLA Ops:
  0.6 0.0 copy-start
  0.6 0.0 copy-start.3
  0.7 0.0 copy-start.2
  0.7 1.0 slice.21
  1.6 2.3 %collective-permute-start = (bf16[8,80]{0,1:T(8,128)(2,1)S(1)}, bf16[8,80]{0,1:T(8,128)(2,1)S(1)}, u32[]{:S(2)}, u32[]{:S(2)}) collective-permute-start(bf16[8,80]{0,1:T(8,128)(2,1)S(1)} %slice.21), channel_id=1, source_target_pairs={{0,1},{1,2},{2,3},{3,4},{4,5},{5,6},{6,7},{7,8},{8,9},{9,10},{10,1... | collective-permute-start | bytes 3848 | tf_op jit(solution)/shard_map/ppermute | solution.py:577
  4.0 0.7 pad.26
  4.7 0.7 reshape.61.mid_dw_ref
  5.5 0.7 reshape.62.last_dw_ref
  6.2 0.8 copy.21.bounds_ref
  6.9 0.0 collective-permute-done
  6.9 1.1 concatenate.9
  8.0 0.1 pad.23
  8.1 0.8 pad_slice_fusion
  8.9 0.2 copy.20
  9.1 1.8 %copy.19 = bf16[1088,84]{1,0:T(8,128)(2,1)} copy(bf16[1088,84]{0,1:T(8,128)(2,1)} %pad_slice_fusion) | data formatting | bytes 365568 | tf_op jit(solution)/shard_map/slice | solution.py:349
  10.9 1.2 reshape.55
  12.2 0.7 fusion.12
  12.9 0.9 reshape.56
  13.8 1.0 slice.31
  14.7 1.0 fusion.9.x_ref
  15.7 0.0 copy-done.3
  15.7 0.0 copy-done.2
  15.8 0.0 copy-start.4
  15.8 0.9 copy-done.4
  16.7 15.6 %subsample.1 = (bf16[128,2560]{1,0:T(8,128)(2,1)S(1)}, bf16[7,128,1024]{2,1,0:T(8,128)(2,1)S(1)}) custom-call(bf16[544,256]{1,0:T(8,128)(2,1)S(1)} %fusion.9.x_ref, f32[344,256]{1,0:T(8,128)S(1)} %pad_convert_fusion.stem_ref, f32[9,256]{1,0:T(8,128)S(1)} %reshape.61.mid_dw_ref, bf16[256,256]{1,0:T(8,128)(2,1)S(1)} %copy-done.3, ...), custom_call_target="tpu_custom_call" | custom-call | flops 20000000000 | bytes 2000000 | tf_op jit(solution)/shard_map/subsample/pallas_call | solution.py:359
  32.3 0.0 copy-start.6
  32.3 1.2 copy-done.6
  33.5 0.0 copy-start.11
  33.5 3.5 %fusion.13 = (f32[128]{0:T(128)S(1)}, f32[128,1024]{1,0:T(8,128)S(1)}) fusion(bf16[128,2560]{1,0:T(8,128)(2,1)S(1)} %get-tuple-element.18, bf16[2560,1024]{1,0:T(8,128)(2,1)} %param.19), kind=kOutput, calls=%fused_computation.31 | convolution fusion | flops 671481728 | bytes 6423040 | tf_op jit(solution)/shard_map/dot_general | solution.py:28
  37.0 0.0 copy-start.8
  37.0 0.2 multiply_reduce_fusion.1
  37.3 0.6 copy-done.8
  37.8 0.0 copy-done.11
  37.8 0.8 multiply_convert_fusion.x_ref
  38.7 16.9 %exchange.1 = bf16[7,128,1024]{2,1,0:T(8,128)(2,1)} custom-call(bf16[128,1024]{1,0:T(8,128)(2,1)} %multiply_convert_fusion.x_ref), custom_call_target="tpu_custom_call" | custom-call | tf_op jit(solution)/shard_map/exchange/pallas_call | solution.py:143
  55.6 1.1 copy.22
  56.7 8.8 %all-to-all-start = ((bf16[128,16,160]{0,2,1:T(8,128)(2,1)}), bf16[128,16,160]{0,2,1:T(8,128)(2,1)}, u32[]{:S(2)}, u32[]{:S(2)}) async-start(bf16[128,16,160]{0,2,1:T(8,128)(2,1)} %bitcast.24), calls=%async_computation | async-start | bytes 1310720 | tf_op jit(solution)/shard_map/all_to_all | solution.py:603
  65.5 0.0 copy-start.7
  65.5 8.6 %convolution_convert_fusion.proj_ref = bf16[896,3072]{1,0:T(8,128)(2,1)S(1)} fusion(bf16[896,1024]{1,0:T(8,128)(2,1)} %bitcast.25, bf16[1024,3072]{1,0:T(8,128)(2,1)} %param.21), kind=kOutput, calls=%fused_computation | convolution fusion | flops 5639897088 | bytes 13631488 | tf_op jit(solution)/shard_map/dot_general | solution.py:28
  74.1 0.0 copy-done
  74.1 0.0 copy-done.7
  74.1 0.0 copy-start.5
  74.1 2.1 %convolution_convert_fusion.1.do_ref = bf16[896,1024]{1,0:T(8,128)(2,1)S(1)} fusion(bf16[896,1024]{1,0:T(8,128)(2,1)S(1)} %bitcast.23, bf16[1024,1024]{1,0:T(8,128)(2,1)S(1)} %copy-done), kind=kOutput, calls=%fused_computation.1 | convolution fusion | flops 1879965696 | bytes 5767168 | tf_op jit(solution)/shard_map/dot_general | solution.py:20
  76.2 0.0 copy-done.5
  76.3 0.0 copy-start.9
  76.3 12.7 %attention.1 = (bf16[128,1024]{1,0:T(8,128)(2,1)S(1)}, bf16[128,3072]{1,0:T(8,128)(2,1)S(1)}) custom-call(bf16[896,3072]{1,0:T(8,128)(2,1)S(1)} %convolution_convert_fusion.proj_ref, bf16[896,1024]{1,0:T(8,128)(2,1)S(1)} %convolution_convert_fusion.1.do_ref, s32[8,2]{1,0:T(8,128)S(1)} %copy.21.bounds_ref, s32[1,7]{1,0:T(1,128)S(1)} %copy-done.5), custom_call_target="tpu_custom_call" | custom-call | flops 20000000000 | bytes 8000000 | tf_op jit(solution)/shard_map/attention/pallas_call | solution.py:536
  88.9 0.0 copy-done.9
  88.9 1.2 fusion.1
  90.1 0.0 all-to-all-done
  90.1 1.1 copy_bitcast_fusion
  91.2 0.0 copy-start.10
  91.3 5.2 %fusion.11 = (f32[128]{0:T(128)S(1)}, f32[128]{0:T(128)S(1)}, f32[128,1024]{1,0:T(8,128)S(1)}) fusion(f32[128]{0:T(128)S(1)} %add_rsqrt_fusion, f32[128,1024]{1,0:T(8,128)} %copy-done.8, f32[128]{0:T(128)S(1)} %broadcast_multiply_fusion.2, f32[1024]{0:T(1024)S(1)} %copy-done.11, bf16[128,3072]{1,0:T(8,128)(2,1)S(1)} %get-tuple-element.19, ...), kind=kOutput, calls=%fused_computation.29 | convolution fusion | flops 806092544 | bytes 8132608 | tf_op jit(solution)/shard_map/dot_general | solution.py:20
  96.5 0.0 copy-done.10
  96.5 0.3 add_convert_fusion.x_ref
  96.8 0.0 copy-start.1
  96.8 27.2 %all_gather.1 = bf16[16,128,1024]{2,1,0:T(8,128)(2,1)S(1)} custom-call(bf16[128,1024]{1,0:T(8,128)(2,1)S(1)} %add_convert_fusion.x_ref), custom_call_target="tpu_custom_call" | custom-call | tf_op jit(solution)/shard_map/all_gather/pallas_call | solution.py:243
  123.9 1.7 %fusion.14 = f32[160,1024]{1,0:T(8,128)} fusion(bf16[2048,160]{0,1:T(8,128)(2,1)S(1)} %copy_bitcast_fusion, bf16[2048,1024]{1,0:T(8,128)(2,1)S(1)} %bitcast.22), kind=kOutput, calls=%fused_computation.32 | convolution fusion | flops 671088640 | bytes 5505024 | tf_op jit(solution)/shard_map/dot_general | solution.py:24
  125.6 0.0 copy-done.1
  (6 shorter events, 0.1 us)
Async XLA Ops:
  0.6 73.5 %copy-start = (bf16[1024,1024]{1,0:T(8,128)(2,1)S(1)}, bf16[1024,1024]{1,0:T(8,128)(2,1)}, u32[]{:S(2)}) copy-start(bf16[1024,1024]{1,0:T(8,128)(2,1)} %param.22) | copy-start | bytes 6291460
  0.6 15.1 %copy-start.3 = (bf16[256,256]{1,0:T(8,128)(2,1)S(1)}, bf16[256,256]{1,0:T(8,128)(2,1)}, u32[]{:S(2)}) copy-start(bf16[256,256]{1,0:T(8,128)(2,1)} %mid_pw_ref.1) | copy-start | bytes 393220
  0.7 15.1 %copy-start.2 = (bf16[128,1024]{1,0:T(8,128)(2,1)S(1)}, bf16[128,1024]{1,0:T(8,128)(2,1)}, u32[]{:S(2)}) copy-start(bf16[128,1024]{1,0:T(8,128)(2,1)} %cot_ref.1) | copy-start | bytes 786436
  1.6 5.3 %collective-permute-start = (bf16[8,80]{0,1:T(8,128)(2,1)S(1)}, bf16[8,80]{0,1:T(8,128)(2,1)S(1)}, u32[]{:S(2)}, u32[]{:S(2)}) collective-permute-start(bf16[8,80]{0,1:T(8,128)(2,1)S(1)} %slice.21), channel_id=1, source_target_pairs={{0,1},{1,2},{2,3},{3,4},{4,5},{5,6},{6,7},{7,8},{8,9},{9,10},{10,1... | collective-permute-start | bytes 3848 | tf_op jit(solution)/shard_map/ppermute | solution.py:577
  15.8 0.9 copy-start.4
  32.3 1.2 copy-start.6
  33.5 4.3 %copy-start.11 = (f32[1024]{0:T(1024)S(1)}, f32[1024]{0:T(1024)}, u32[]{:S(2)}) copy-start(f32[1024]{0:T(1024)} %param.20) | copy-start | bytes 12292
  37.0 0.8 copy-start.8
  56.7 33.4 %all-to-all-start = ((bf16[128,16,160]{0,2,1:T(8,128)(2,1)}), bf16[128,16,160]{0,2,1:T(8,128)(2,1)}, u32[]{:S(2)}, u32[]{:S(2)}) async-start(bf16[128,16,160]{0,2,1:T(8,128)(2,1)} %bitcast.24), calls=%async_computation | async-start | bytes 1310720 | tf_op jit(solution)/shard_map/all_to_all | solution.py:603
  65.5 8.7 %copy-start.7 = (bf16[7,128,1024]{2,1,0:T(8,128)(2,1)S(1)}, bf16[7,128,1024]{2,1,0:T(8,128)(2,1)}, u32[]{:S(2)}) copy-start(bf16[7,128,1024]{2,1,0:T(8,128)(2,1)} %copy-done.6) | copy-start | bytes 5505028
  74.1 2.1 %copy-start.5 = (s32[1,7]{1,0:T(1,128)S(1)}, s32[1,7]{1,0:T(1,128)}, u32[]{:S(2)}) copy-start(s32[1,7]{1,0:T(1,128)} %live_ref.1) | copy-start | bytes 88
  76.3 12.7 %copy-start.9 = (f32[128,1024]{1,0:T(8,128)S(1)}, f32[128,1024]{1,0:T(8,128)}, u32[]{:S(2)}) copy-start(f32[128,1024]{1,0:T(8,128)} %copy-done.8) | copy-start | bytes 1572868
  91.2 5.2 %copy-start.10 = (f32[128,1024]{1,0:T(8,128)S(1)}, f32[128,1024]{1,0:T(8,128)}, u32[]{:S(2)}) copy-start(f32[128,1024]{1,0:T(8,128)} %copy-done.8) | copy-start | bytes 1572868
  96.8 28.9 %copy-start.1 = (bf16[128,1024]{1,0:T(8,128)(2,1)}, bf16[128,1024]{1,0:T(8,128)(2,1)S(1)}, u32[]{:S(2)}) copy-start(bf16[128,1024]{1,0:T(8,128)(2,1)S(1)} %add_convert_fusion.x_ref) | copy-start | bytes 786436

commit v4 on v3

--- a/solution.py
+++ b/solution.py
@@ -270,6 +270,7 @@
     odd,
     second,
     shifted,
+    taps_ref,
     send,
     recv,
 ):
@@ -281,8 +282,17 @@
     span = shifted.shape[1] - 256
     odd[0] = jnp.zeros(odd.shape[1:], odd.dtype)
     second[0] = jnp.zeros(second.shape[1:], second.dtype)
-    for i in range(4):
-        shifted[i] = stem_ref[8 - 2 * i : 8 - 2 * i + span + 256, :]
+    shifted[...] = jnp.zeros(shifted.shape, jnp.float32)
+    for dt in range(3):
+        for df in range(3):
+            row = 3 * dt + df
+            tap = stem_ref[dt, df : df + 1, :].astype(jnp.float32)
+            for i in range(4):
+                at = span + 2 * i + dt * MEL_PITCH + df
+                shifted[i, at : at + 1, :] = tap
+            taps_ref[row : row + 1, :] = mid_dw_ref[dt, df : df + 1, :].astype(jnp.float32)
+            last = last_dw_ref[dt, df : df + 1, :].astype(jnp.float32)
+            taps_ref[16 + row : 17 + row, :] = last
 
     def step(k, half):
         def stem(i):
@@ -299,7 +309,7 @@
         for df in range(3):
             src = parts[df]
             for dt in range(3):
-                tap = mid_dw_ref[3 * dt + df : 3 * dt + df + 1, :]
+                tap = taps_ref[3 * dt + df : 3 * dt + df + 1, :]
                 phase = (3, 0, 1)[dt]
                 start = 7 if dt == 0 else 8
                 early += src[phase, start : start + main, :] * tap
@@ -319,7 +329,7 @@
         total = jnp.zeros((main, 256), jnp.float32)
         for df in range(3):
             for dt in range(3):
-                tap = last_dw_ref[3 * dt + df : 3 * dt + df + 1, :]
+                tap = taps_ref[16 + 3 * dt + df : 17 + 3 * dt + df, :]
                 phase = (1, 0, 1)[dt]
                 start = 7 if dt == 0 else 8
                 total += second[2 * f + df, phase, start : start + main, :] * tap
@@ -344,18 +354,15 @@
     rows = main + 8
     channels = stem_kernel.shape[-1]
     mids = mel // 4
-    series = jnp.concatenate([jnp.zeros((56, mel), features.dtype), halo, features], axis=0)
+    blank = jnp.zeros((57, mel), features.dtype)
+    series = jnp.concatenate([blank, halo, features, blank[:7]], axis=0)
     series = jnp.pad(series, ((0, 0), (1, MEL_PITCH - mel - 1)))
-    late = jnp.pad(series, ((1, 0), (0, 0)))[:-1].reshape(rows, 8 * MEL_PITCH)
-    tail = series.reshape(rows, 8 * MEL_PITCH)[:, 7 * MEL_PITCH :]
-    wide = jnp.concatenate([late, tail], axis=1)
+    eights = series.reshape(rows + 1, 8 * MEL_PITCH)
+    wide = jnp.concatenate([eights[:-1], eights[1:, :MEL_PITCH]], axis=1)
     x = jnp.concatenate(
         [wide[:, 2 * p * MEL_PITCH : (2 * p + 3) * MEL_PITCH] for p in range(4)], axis=0
     )
     x = jnp.pad(x, ((0, 0), (0, 256 - 3 * MEL_PITCH)))
-    base = jnp.pad(stem_kernel.astype(jnp.float32), ((0, 0), (0, MEL_PITCH - 3), (0, 0)))
-    base = base.reshape(3 * MEL_PITCH, channels)
-    base = jnp.pad(base, ((mel + 8, 256 - 3 * MEL_PITCH), (0, 0)))
     return pl.pallas_call(
         functools.partial(subsample_kernel, size),
         out_shape=(
@@ -369,6 +376,7 @@
             pltpu.VMEM((2, 4, rows, channels), jnp.float32),
             pltpu.VMEM((mids + 1, 2, rows, channels), jnp.float32),
             pltpu.VMEM((4, mel + 256, channels), jnp.float32),
+            pltpu.VMEM((32, channels), jnp.float32),
         ]
         + EXCHANGE_SEMS,
         compiler_params=pltpu.CompilerParams(
@@ -380,10 +388,10 @@
         name="subsample",
     )(
         x,
-        base,
-        mid_depthwise.reshape(9, channels).astype(jnp.float32),
+        stem_kernel,
+        mid_depthwise,
         mid_pointwise,
-        last_depthwise.reshape(9, channels).astype(jnp.float32),
+        last_depthwise,
         last_pointwise,
         cotangent,
     )

time: 126 us -> 119 us (0.944)
  local copies, waits for them, and re-layouts: 16.6 us -> 10.4 us
  Pallas kernels: 72.4 us -> 75.5 us
  matrix products: 22.3 us -> 19.8 us
  starting transfers between devices: 11.1 us -> 9.2 us
    dot_general x3, matrix products: 13.3 us -> 10.7 us  [dot_nn(): return jnp.dot(a, b, preferred_element_type=jnp.float32)]
    pallas_call x1, Pallas kernels: 15.6 us -> 18.1 us  [subsample(): pl.pallas_call(functools.partial(subsample_kernel, size), out_shape=(jax....]
    all_to_all x1, starting transfers between devices: 8.76 us -> 6.85 us  [per_device(): columns = lax.all_to_all(flat_sent[:, :own_cols], 'tm', 1, 0, tiled=True)]
    reshape x3 -> x1, local copies, waits for them, and re-layouts: 2.13 us -> 0.24 us  [subsample(): eights = series.reshape(rows + 1, 8 * MEL_PITCH)]
    slice x3 -> x5, local copies, waits for them, and re-layouts: 3.59 us -> 2.11 us  [the longest x4 2.11 us: subsample(): wide = jnp.concatenate([eights[:-1], eights[1:, :MEL_PITCH]], axis=1)]
    convert_element_type x2 -> x0, local copies, waits for them, and re-layouts: 1.41 us -> none  [the longest x1 0.7 us: subsample(): mid_depthwise.reshape(9, channels).astype(jnp.float32)]
    unnamed x25 -> x36, local copies, waits for them, and re-layouts: 3.52 us -> 2.87 us
  transfers between devices with their start and end apart: 2 -> 2, of which waited for: 0 -> 1; matrix products, arithmetic and copies ran while one was open for 12% -> 11% of each run, Pallas kernels for 10% -> 11%
where the time goes in v4:
time: 119 us; the launch traced here: 118 us
  Pallas kernels  75.5 us (63%)
  matrix products  19.8 us (17%)
  local copies, waits for them, and re-layouts  10.4 us (9%)
  starting transfers between devices  9.2 us (8%)
  other arithmetic  2.47 us (2%)
    pallas_call x1, Pallas kernels, gathered(): pl.pallas_call(functools.partial(gather_kernel, size), out_shape=jax.Shap...  27.1 us
    pallas_call x1, Pallas kernels, subsample(): pl.pallas_call(functools.partial(subsample_kernel, size), out_shape=(jax....  18.1 us
    pallas_call x1, Pallas kernels, gathered_window(): pl.pallas_call(functools.partial(exchange_kernel, size), out_shape=jax.Sh...  17.6 us
    pallas_call x1, Pallas kernels, attention(): pl.pallas_call(functools.partial(attention_kernel, size), out_shape=(jax....  12.6 us
    dot_general x3, matrix products, dot_nn(): return jnp.dot(a, b, preferred_element_type=jnp.float32)  10.7 us
    dot_general x2, matrix products, dot_nt(): lax.dot_general(a, b, (((1,), (1,)), ((), ())), preferred_element_type=jn...  7.32 us
    all_to_all x1, starting transfers between devices, per_device(): columns = lax.all_to_all(flat_sent[:, :own_cols], 'tm', 1, 0, tiled=True)  6.85 us
    unnamed x36, local copies, waits for them, and re-layouts  2.87 us
  transfers between devices with their start and end apart: 2, of which 1 were waited for; matrix products, arithmetic and copies ran while one was open for 11% of the time, Pallas kernels for 11%

profile of v4, /device:TPU:0, one launch (start us, length us, event | category | flops | bytes accessed | tf_op | source)
XLA Modules:
  0.0 118.4 jit_solution(915705322051919807)
XLA Ops:
  0.6 0.0 copy-start
  0.6 0.0 copy-start.5
  0.7 0.0 copy-start.6
  0.7 0.0 copy-start.3
  0.7 0.0 copy-start.7
  0.7 0.0 copy-start.4
  0.7 0.0 copy-start.2
  0.7 1.0 slice.27
  1.7 2.3 %collective-permute-start = (bf16[8,80]{0,1:T(8,128)(2,1)S(1)}, bf16[8,80]{0,1:T(8,128)(2,1)S(1)}, u32[]{:S(2)}, u32[]{:S(2)}) collective-permute-start(bf16[8,80]{0,1:T(8,128)(2,1)S(1)} %slice.27), channel_id=1, source_target_pairs={{0,1},{1,2},{2,3},{3,4},{4,5},{5,6},{6,7},{7,8},{8,9},{9,10},{10,1... | collective-permute-start | bytes 3848 | tf_op jit(solution)/shard_map/ppermute | solution.py:585
  4.0 0.8 copy.21.bounds_ref
  4.8 0.1 collective-permute-done
  4.9 1.1 concatenate.9
  6.0 0.7 pad_slice_fusion
  6.7 0.2 copy.26
  6.9 1.1 copy.19
  8.1 0.2 slice.30
  8.3 0.8 fusion.12
  9.0 0.1 pad.8.clone
  9.2 0.2 reshape.43
  9.4 0.0 slice-start
  9.5 1.2 fusion.9.x_ref
  10.6 0.0 copy-done.5
  10.7 0.0 copy-done.6
  10.7 0.0 copy-done.3
  10.7 0.0 copy-done.7
  10.7 0.0 copy-done.4
  10.7 0.0 copy-done.2
  10.7 0.0 slice-start.1
  10.7 18.1 %subsample.1 = (bf16[128,2560]{1,0:T(8,128)(2,1)S(1)}, bf16[7,128,1024]{2,1,0:T(8,128)(2,1)S(1)}) custom-call(bf16[544,256]{1,0:T(8,128)(2,1)S(1)} %fusion.9.x_ref, bf16[3,3,256]{2,1,0:T(4,128)(2,1)S(1)} %copy-done.5, bf16[3,3,256]{2,1,0:T(4,128)(2,1)S(1)} %copy-done.6, bf16[256,256]{1,0:T(8,128)(2,1)S(1)} %copy-done.3, bf16[3,3,256]{2,1,0:T(4,128)(2,1)S(1)} %copy-done.7, ...), custom_call_target="tpu_custom_call" | custom-call | flops 20000000000 | bytes 2000000 | tf_op jit(solution)/shard_map/subsample/pallas_call | solution.py:366
  28.8 0.0 copy-start.9
  28.9 1.3 %copy-done.9 = bf16[7,128,1024]{2,1,0:T(8,128)(2,1)} copy-done((bf16[7,128,1024]{2,1,0:T(8,128)(2,1)}, bf16[7,128,1024]{2,1,0:T(8,128)(2,1)S(1)}, u32[]{:S(2)}) %copy-start.9) | copy-done | bytes 1835032
  30.1 0.0 copy-start.14
  30.1 0.0 slice-done
  30.1 0.0 slice-done.1
  30.1 0.9 fusion.13
  31.1 0.0 copy-start.11
  31.1 0.2 multiply_reduce_fusion.1
  31.3 0.6 copy-done.11
  31.9 0.0 copy-done.14
  31.9 0.8 multiply_convert_fusion.x_ref
  32.7 17.6 %exchange.1 = bf16[7,128,1024]{2,1,0:T(8,128)(2,1)} custom-call(bf16[128,1024]{1,0:T(8,128)(2,1)} %multiply_convert_fusion.x_ref), custom_call_target="tpu_custom_call" | custom-call | tf_op jit(solution)/shard_map/exchange/pallas_call | solution.py:143
  50.3 1.1 copy.22
  51.4 6.8 %all-to-all-start = ((bf16[128,16,160]{0,2,1:T(8,128)(2,1)}), bf16[128,16,160]{0,2,1:T(8,128)(2,1)}, u32[]{:S(2)}, u32[]{:S(2)}) async-start(bf16[128,16,160]{0,2,1:T(8,128)(2,1)} %bitcast.26), calls=%async_computation | async-start | bytes 1310720 | tf_op jit(solution)/shard_map/all_to_all | solution.py:611
  58.3 0.0 copy-start.10
  58.3 8.6 %convolution_convert_fusion.proj_ref = bf16[896,3072]{1,0:T(8,128)(2,1)S(1)} fusion(bf16[896,1024]{1,0:T(8,128)(2,1)} %bitcast.27, bf16[1024,3072]{1,0:T(8,128)(2,1)} %param.21), kind=kOutput, calls=%fused_computation | convolution fusion | flops 5639897088 | bytes 13631488 | tf_op jit(solution)/shard_map/dot_general | solution.py:28
  66.9 0.0 copy-done
  66.9 0.0 copy-done.10
  66.9 0.0 copy-start.8
  66.9 2.1 %convolution_convert_fusion.1.do_ref = bf16[896,1024]{1,0:T(8,128)(2,1)S(1)} fusion(bf16[896,1024]{1,0:T(8,128)(2,1)S(1)} %bitcast.23, bf16[1024,1024]{1,0:T(8,128)(2,1)S(1)} %copy-done), kind=kOutput, calls=%fused_computation.1 | convolution fusion | flops 1879965696 | bytes 5767168 | tf_op jit(solution)/shard_map/dot_general | solution.py:20
  69.0 0.0 copy-done.8
  69.1 0.0 copy-start.12
  69.1 12.6 %attention.1 = (bf16[128,1024]{1,0:T(8,128)(2,1)S(1)}, bf16[128,3072]{1,0:T(8,128)(2,1)S(1)}) custom-call(bf16[896,3072]{1,0:T(8,128)(2,1)S(1)} %convolution_convert_fusion.proj_ref, bf16[896,1024]{1,0:T(8,128)(2,1)S(1)} %convolution_convert_fusion.1.do_ref, s32[8,2]{1,0:T(8,128)S(1)} %copy.21.bounds_ref, s32[1,7]{1,0:T(1,128)S(1)} %copy-done.8), custom_call_target="tpu_custom_call" | custom-call | flops 20000000000 | bytes 8000000 | tf_op jit(solution)/shard_map/attention/pallas_call | solution.py:544
  81.7 0.0 copy-done.12
  81.7 1.2 fusion.1
  82.9 0.0 all-to-all-done
  82.9 1.1 copy_bitcast_fusion
  84.0 0.0 copy-start.13
  84.1 5.2 %fusion.11 = (f32[128]{0:T(128)S(1)}, f32[128]{0:T(128)S(1)}, f32[128,1024]{1,0:T(8,128)S(1)}) fusion(f32[128]{0:T(128)S(1)} %add_rsqrt_fusion, f32[128,1024]{1,0:T(8,128)} %copy-done.11, f32[128]{0:T(128)S(1)} %broadcast_multiply_fusion.2, f32[1024]{0:T(1024)S(1)} %copy-done.14, bf16[128,3072]{1,0:T(8,128)(2,1)S(1)} %get-tuple-element.19, ...), kind=kOutput, calls=%fused_computation.28 | convolution fusion | flops 806092544 | bytes 8132608 | tf_op jit(solution)/shard_map/dot_general | solution.py:20
  89.3 0.0 copy-done.13
  89.3 0.2 add_convert_fusion.x_ref
  89.5 0.0 copy-start.1
  89.6 27.1 %all_gather.1 = bf16[16,128,1024]{2,1,0:T(8,128)(2,1)S(1)} custom-call(bf16[128,1024]{1,0:T(8,128)(2,1)S(1)} %add_convert_fusion.x_ref), custom_call_target="tpu_custom_call" | custom-call | tf_op jit(solution)/shard_map/all_gather/pallas_call | solution.py:243
  116.7 1.7 %fusion.14 = f32[160,1024]{1,0:T(8,128)} fusion(bf16[2048,160]{0,1:T(8,128)(2,1)S(1)} %copy_bitcast_fusion, bf16[2048,1024]{1,0:T(8,128)(2,1)S(1)} %bitcast.22), kind=kOutput, calls=%fused_computation.31 | convolution fusion | flops 671088640 | bytes 5505024 | tf_op jit(solution)/shard_map/dot_general | solution.py:24
  118.4 0.0 copy-done.1
  (7 shorter events, 0.0 us)
Async XLA Ops:
  0.6 66.3 %copy-start = (bf16[1024,1024]{1,0:T(8,128)(2,1)S(1)}, bf16[1024,1024]{1,0:T(8,128)(2,1)}, u32[]{:S(2)}) copy-start(bf16[1024,1024]{1,0:T(8,128)(2,1)} %param.22) | copy-start | bytes 6291460
  0.6 10.0 %copy-start.5 = (bf16[3,3,256]{2,1,0:T(4,128)(2,1)S(1)}, bf16[3,3,256]{2,1,0:T(4,128)(2,1)}, u32[]{:S(2)}) copy-start(bf16[3,3,256]{2,1,0:T(4,128)(2,1)} %stem_ref.1) | copy-start | bytes 13828
  0.7 10.0 %copy-start.6 = (bf16[3,3,256]{2,1,0:T(4,128)(2,1)S(1)}, bf16[3,3,256]{2,1,0:T(4,128)(2,1)}, u32[]{:S(2)}) copy-start(bf16[3,3,256]{2,1,0:T(4,128)(2,1)} %mid_dw_ref.1) | copy-start | bytes 13828
  0.7 10.0 %copy-start.3 = (bf16[256,256]{1,0:T(8,128)(2,1)S(1)}, bf16[256,256]{1,0:T(8,128)(2,1)}, u32[]{:S(2)}) copy-start(bf16[256,256]{1,0:T(8,128)(2,1)} %mid_pw_ref.1) | copy-start | bytes 393220
  0.7 10.0 %copy-start.7 = (bf16[3,3,256]{2,1,0:T(4,128)(2,1)S(1)}, bf16[3,3,256]{2,1,0:T(4,128)(2,1)}, u32[]{:S(2)}) copy-start(bf16[3,3,256]{2,1,0:T(4,128)(2,1)} %last_dw_ref.1) | copy-start | bytes 13828
  0.7 10.0 %copy-start.4 = (bf16[256,256]{1,0:T(8,128)(2,1)S(1)}, bf16[256,256]{1,0:T(8,128)(2,1)}, u32[]{:S(2)}) copy-start(bf16[256,256]{1,0:T(8,128)(2,1)} %last_pw_ref.1) | copy-start | bytes 393220
  0.7 10.0 %copy-start.2 = (bf16[128,1024]{1,0:T(8,128)(2,1)S(1)}, bf16[128,1024]{1,0:T(8,128)(2,1)}, u32[]{:S(2)}) copy-start(bf16[128,1024]{1,0:T(8,128)(2,1)} %cot_ref.1) | copy-start | bytes 786436
  1.7 3.2 %collective-permute-start = (bf16[8,80]{0,1:T(8,128)(2,1)S(1)}, bf16[8,80]{0,1:T(8,128)(2,1)S(1)}, u32[]{:S(2)}, u32[]{:S(2)}) collective-permute-start(bf16[8,80]{0,1:T(8,128)(2,1)S(1)} %slice.27), channel_id=1, source_target_pairs={{0,1},{1,2},{2,3},{3,4},{4,5},{5,6},{6,7},{7,8},{8,9},{9,10},{10,1... | collective-permute-start | bytes 3848 | tf_op jit(solution)/shard_map/ppermute | solution.py:585
  9.4 20.7 %slice-start = ((s8[5242880]{0:T(1024)(128)(4,1)}), s8[4194304]{0:T(1024)(128)(4,1)S(1)}, s32[]{:S(2)}) async-start(s8[5242880]{0:T(1024)(128)(4,1)} %bitcast.24), calls=%async_computation.1 | async-start | bytes 8388608
  10.7 19.4 %slice-start.1 = ((s8[5242880]{0:T(1024)(128)(4,1)}), s8[1048576]{0:T(1024)(128)(4,1)S(1)}, s32[]{:S(2)}) async-start(s8[5242880]{0:T(1024)(128)(4,1)} %bitcast.24), calls=%async_computation.2 | async-start | bytes 2097152
  28.8 1.3 %copy-start.9 = (bf16[7,128,1024]{2,1,0:T(8,128)(2,1)}, bf16[7,128,1024]{2,1,0:T(8,128)(2,1)S(1)}, u32[]{:S(2)}) copy-start(bf16[7,128,1024]{2,1,0:T(8,128)(2,1)S(1)} %get-tuple-element.13) | copy-start | bytes 5505028
  30.1 1.8 %copy-start.14 = (f32[1024]{0:T(1024)S(1)}, f32[1024]{0:T(1024)}, u32[]{:S(2)}) copy-start(f32[1024]{0:T(1024)} %param.20) | copy-start | bytes 12292
  31.1 0.8 copy-start.11
  51.4 31.5 %all-to-all-start = ((bf16[128,16,160]{0,2,1:T(8,128)(2,1)}), bf16[128,16,160]{0,2,1:T(8,128)(2,1)}, u32[]{:S(2)}, u32[]{:S(2)}) async-start(bf16[128,16,160]{0,2,1:T(8,128)(2,1)} %bitcast.26), calls=%async_computation | async-start | bytes 1310720 | tf_op jit(solution)/shard_map/all_to_all | solution.py:611
  58.3 8.7 %copy-start.10 = (bf16[7,128,1024]{2,1,0:T(8,128)(2,1)S(1)}, bf16[7,128,1024]{2,1,0:T(8,128)(2,1)}, u32[]{:S(2)}) copy-start(bf16[7,128,1024]{2,1,0:T(8,128)(2,1)} %copy-done.9) | copy-start | bytes 5505028
  66.9 2.1 %copy-start.8 = (s32[1,7]{1,0:T(1,128)S(1)}, s32[1,7]{1,0:T(1,128)}, u32[]{:S(2)}) copy-start(s32[1,7]{1,0:T(1,128)} %live_ref.1) | copy-start | bytes 88
  69.1 12.7 %copy-start.12 = (f32[128,1024]{1,0:T(8,128)S(1)}, f32[128,1024]{1,0:T(8,128)}, u32[]{:S(2)}) copy-start(f32[128,1024]{1,0:T(8,128)} %copy-done.11) | copy-start | bytes 1572868
  84.0 5.2 %copy-start.13 = (f32[128,1024]{1,0:T(8,128)S(1)}, f32[128,1024]{1,0:T(8,128)}, u32[]{:S(2)}) copy-start(f32[128,1024]{1,0:T(8,128)} %copy-done.11) | copy-start | bytes 1572868
  89.5 28.9 %copy-start.1 = (bf16[128,1024]{1,0:T(8,128)(2,1)}, bf16[128,1024]{1,0:T(8,128)(2,1)S(1)}, u32[]{:S(2)}) copy-start(bf16[128,1024]{1,0:T(8,128)(2,1)S(1)} %add_convert_fusion.x_ref) | copy-start | bytes 786436

commit v5 on v4

--- a/solution.py
+++ b/solution.py
@@ -132,24 +132,30 @@
 EXCHANGE_SEMS = [pltpu.SemaphoreType.DMA((7,)), pltpu.SemaphoreType.DMA((6,))]
 
 
-def exchange_kernel(size, x_ref, out_ref, send, recv):
+def exchange_kernel(size, x_ref, cot_ref, weight_ref, out_ref, do_ref, send, recv):
     exchange = Exchange(size, x_ref, out_ref, send, recv)
     exchange.begin()
+    do_ref[...] = dot_nt(cot_ref[...], weight_ref[...]).astype(jnp.bfloat16)
     exchange.forward()
     exchange.finish()
 
 
-def gathered_window(x, size):
-    out = pl.pallas_call(
+def gathered_window(x, cot_window, out_weight, size):
+    out, d_attention = pl.pallas_call(
         functools.partial(exchange_kernel, size),
-        out_shape=jax.ShapeDtypeStruct((7,) + x.shape, x.dtype),
-        in_specs=[pl.BlockSpec(memory_space=pltpu.VMEM)],
-        out_specs=pl.BlockSpec(memory_space=pltpu.VMEM),
+        out_shape=(
+            jax.ShapeDtypeStruct((7,) + x.shape, x.dtype),
+            jax.ShapeDtypeStruct(cot_window.shape, x.dtype),
+        ),
+        in_specs=[pl.BlockSpec(memory_space=pltpu.VMEM)] * 3,
+        out_specs=(pl.BlockSpec(memory_space=pltpu.VMEM),) * 2,
         scratch_shapes=EXCHANGE_SEMS,
-        compiler_params=pltpu.CompilerParams(collective_id=1, has_side_effects=True),
+        compiler_params=pltpu.CompilerParams(
+            vmem_limit_bytes=32 * 1024 * 1024, collective_id=1, has_side_effects=True
+        ),
         name="exchange",
-    )(x)
-    return out.reshape((7 * x.shape[0],) + x.shape[1:])
+    )(x, cot_window, out_weight)
+    return out.reshape((7 * x.shape[0],) + x.shape[1:]), d_attention
 
 
 def gather_kernel(size, x_ref, out_ref, send, recv, side_send, side_recv, own_sem):
@@ -603,13 +609,10 @@
     inv_std = lax.rsqrt(jnp.mean(centered * centered, axis=-1, keepdims=True) + norm_eps)
     normalized = centered * inv_std
     normed = (normalized * norm_gain).astype(jnp.bfloat16)
-    normed_window = gathered_window(normed, size)
-    normed_window, flat_sent, cot_window = lax.optimization_barrier(
-        (normed_window, flat_rows, cot_window)
-    )
+    normed_window, d_attention = gathered_window(normed, cot_window, out_weight, size)
+    normed_window, flat_sent = lax.optimization_barrier((normed_window, flat_rows))
     own_cols = size * (flat_rows.shape[1] // size)
     columns = lax.all_to_all(flat_sent[:, :own_cols], "tm", 1, 0, tiled=True)
-    d_attention = dot_nt(cot_window, out_weight).astype(jnp.bfloat16)
     projected = dot_nn(normed_window, qkv_weight).astype(jnp.bfloat16)
     mixed, grads = attention(size, projected, d_attention, utt_bounds, live_blocks)
     grads, columns = lax.optimization_barrier((grads, columns))

time: 119 us -> 119 us (level)
  local copies, waits for them, and re-layouts: 10.4 us -> 13.5 us
  Pallas kernels: 75.5 us -> 73.4 us
  other arithmetic: 2.47 us -> 0.72 us
    unnamed x36 -> x30, local copies, waits for them, and re-layouts: 2.87 us -> 8.3 us
    dot_general x3, matrix products: 10.7 us -> 13.4 us  [dot_nn(): return jnp.dot(a, b, preferred_element_type=jnp.float32)]
    dot_general x2 -> x1, matrix products: 7.32 us -> 5.09 us  [dot_nt(): lax.dot_general(a, b, (((1,), (1,)), ((), ())), preferred_element_type=jn...]
    pallas_call x1, Pallas kernels: 17.6 us -> 15.6 us  [gathered_window(): pl.pallas_call(functools.partial(exchange_kernel, size), out_shape=(jax.S...]
    slice x4, local copies, waits for them, and re-layouts: 2.11 us -> 0.49 us  [subsample(): wide = jnp.concatenate([eights[:-1], eights[1:, :MEL_PITCH]], axis=1)]
  transfers between devices with their start and end apart: 2 -> 2, of which waited for: 1 -> 1; matrix products, arithmetic and copies ran while one was open for 11% -> 9% of each run, Pallas kernels for 11% -> 11%
where the time goes in v5:
time: 119 us; the launch traced here: 118 us
  Pallas kernels  73.4 us (62%)
  matrix products  20.2 us (17%)
  local copies, waits for them, and re-layouts  13.5 us (11%)
  starting transfers between devices  9.16 us (8%)
    pallas_call x1, Pallas kernels, gathered(): pl.pallas_call(functools.partial(gather_kernel, size), out_shape=jax.Shap...  27.2 us
    pallas_call x1, Pallas kernels, subsample(): pl.pallas_call(functools.partial(subsample_kernel, size), out_shape=(jax....  18 us
    pallas_call x1, Pallas kernels, gathered_window(): pl.pallas_call(functools.partial(exchange_kernel, size), out_shape=(jax.S...  15.6 us
    dot_general x3, matrix products, dot_nn(): return jnp.dot(a, b, preferred_element_type=jnp.float32)  13.4 us
    pallas_call x1, Pallas kernels, attention(): pl.pallas_call(functools.partial(attention_kernel, size), out_shape=(jax....  12.6 us
    unnamed x30, local copies, waits for them, and re-layouts  8.3 us
    all_to_all x1, starting transfers between devices, per_device(): columns = lax.all_to_all(flat_sent[:, :own_cols], 'tm', 1, 0, tiled=True)  6.82 us
    dot_general x1, matrix products, dot_nt(): lax.dot_general(a, b, (((1,), (1,)), ((), ())), preferred_element_type=jn...  5.09 us
  transfers between devices with their start and end apart: 2, of which 1 were waited for; matrix products, arithmetic and copies ran while one was open for 9% of the time, Pallas kernels for 11%

profile of v5, /device:TPU:0, one launch (start us, length us, event | category | flops | bytes accessed | tf_op | source)
XLA Modules:
  0.0 117.9 jit_solution(3166874707057862059)
XLA Ops:
  0.6 0.8 slice.27
  1.4 2.3 %collective-permute-start = (bf16[8,80]{0,1:T(8,128)(2,1)S(1)}, bf16[8,80]{0,1:T(8,128)(2,1)S(1)}, u32[]{:S(2)}, u32[]{:S(2)}) collective-permute-start(bf16[8,80]{0,1:T(8,128)(2,1)S(1)} %slice.27), channel_id=1, source_target_pairs={{0,1},{1,2},{2,3},{3,4},{4,5},{5,6},{6,7},{7,8},{8,9},{9,10},{10,1... | collective-permute-start | bytes 3848 | tf_op jit(solution)/shard_map/ppermute | solution.py:591
  3.8 0.8 copy.21.bounds_ref
  4.5 0.1 collective-permute-done
  4.6 1.1 concatenate.9
  5.7 0.1 pad_slice_fusion
  5.8 0.2 copy.26
  6.0 0.2 copy.19
  6.2 0.2 slice.30
  6.4 0.1 fusion.12
  6.6 0.1 pad.8.clone
  6.7 0.2 reshape.43
  7.0 0.1 fusion.9.x_ref
  7.1 0.0 copy-start.2
  7.1 0.9 copy-done.2
  8.0 0.0 copy-start.7
  8.0 0.9 copy-done.7
  8.9 0.0 copy-start.8
  8.9 0.9 copy-done.8
  9.8 0.0 copy-start.9
  9.8 0.7 copy-done.9
  10.5 0.0 copy-start.10
  10.5 0.7 copy-done.10
  11.2 0.0 copy-start.11
  11.2 0.7 copy-done.11
  11.9 18.0 %subsample.1 = (bf16[128,2560]{1,0:T(8,128)(2,1)S(1)}, bf16[7,128,1024]{2,1,0:T(8,128)(2,1)S(1)}) custom-call(bf16[544,256]{1,0:T(8,128)(2,1)S(1)} %fusion.9.x_ref, bf16[3,3,256]{2,1,0:T(4,128)(2,1)S(1)} %copy-done.9, bf16[3,3,256]{2,1,0:T(4,128)(2,1)S(1)} %copy-done.10, bf16[256,256]{1,0:T(8,128)(2,1)S(1)} %copy-done.7, bf16[3,3,256]{2,1,0:T(4,128)(2,1)S(1)} %copy-done.11, ...), custom_call_target="tpu_custom_call" | custom-call | flops 20000000000 | bytes 2000000 | tf_op jit(solution)/shard_map/subsample/pallas_call | solution.py:372
  29.9 0.0 copy-start.13
  29.9 0.0 copy-start
  29.9 3.6 %fusion.13 = (f32[128]{0:T(128)S(1)}, f32[128,1024]{1,0:T(8,128)S(1)}) fusion(bf16[128,2560]{1,0:T(8,128)(2,1)S(1)} %get-tuple-element.20, bf16[2560,1024]{1,0:T(8,128)(2,1)} %param.19), kind=kOutput, calls=%fused_computation.29 | convolution fusion | flops 671481728 | bytes 6423040 | tf_op jit(solution)/shard_map/dot_general | solution.py:28
  33.6 0.2 multiply_reduce_fusion.1
  33.8 0.0 copy-done.13
  33.8 0.1 multiply_convert_fusion.x_ref
  33.9 0.0 copy-done
  33.9 15.6 %exchange.1 = (bf16[7,128,1024]{2,1,0:T(8,128)(2,1)S(1)}, bf16[896,1024]{1,0:T(8,128)(2,1)S(1)}) custom-call(bf16[128,1024]{1,0:T(8,128)(2,1)S(1)} %multiply_convert_fusion.x_ref, bf16[896,1024]{1,0:T(8,128)(2,1)S(1)} %bitcast.21, bf16[1024,1024]{1,0:T(8,128)(2,1)S(1)} %copy-done), custom_call_target="tpu_custom_call" | custom-call | tf_op jit(solution)/shard_map/exchange/pallas_call | solution.py:144
  49.6 0.0 copy-start.4
  49.6 1.2 %copy-done.4 = bf16[896,1024]{1,0:T(8,128)(2,1)} copy-done((bf16[896,1024]{1,0:T(8,128)(2,1)}, bf16[896,1024]{1,0:T(8,128)(2,1)S(1)}, u32[]{:S(2)}) %copy-start.4) | copy-done | bytes 1835032
  50.8 0.0 copy-start.6
  50.8 1.2 %copy-done.6 = bf16[7,128,1024]{2,1,0:T(8,128)(2,1)} copy-done((bf16[7,128,1024]{2,1,0:T(8,128)(2,1)}, bf16[7,128,1024]{2,1,0:T(8,128)(2,1)S(1)}, u32[]{:S(2)}) %copy-start.6) | copy-done | bytes 1835032
  52.0 1.1 copy.22
  53.1 6.8 %all-to-all-start = ((bf16[128,16,160]{0,2,1:T(8,128)(2,1)}), bf16[128,16,160]{0,2,1:T(8,128)(2,1)}, u32[]{:S(2)}, u32[]{:S(2)}) async-start(bf16[128,16,160]{0,2,1:T(8,128)(2,1)} %bitcast.23), calls=%async_computation | async-start | bytes 1310720 | tf_op jit(solution)/shard_map/all_to_all | solution.py:615
  59.9 0.0 copy-start.5
  60.0 0.0 copy-start.12
  60.0 8.6 %convolution_convert_fusion.proj_ref = bf16[896,3072]{1,0:T(8,128)(2,1)S(1)} fusion(bf16[896,1024]{1,0:T(8,128)(2,1)} %bitcast.22, bf16[1024,3072]{1,0:T(8,128)(2,1)} %param.21), kind=kOutput, calls=%fused_computation | convolution fusion | flops 5639897088 | bytes 13631488 | tf_op jit(solution)/shard_map/dot_general | solution.py:28
  68.6 0.0 copy-done.5
  68.6 0.0 copy-done.12
  68.6 12.6 %attention.1 = (bf16[128,1024]{1,0:T(8,128)(2,1)S(1)}, bf16[128,3072]{1,0:T(8,128)(2,1)S(1)}) custom-call(bf16[896,3072]{1,0:T(8,128)(2,1)S(1)} %convolution_convert_fusion.proj_ref, bf16[896,1024]{1,0:T(8,128)(2,1)S(1)} %copy-done.5, s32[8,2]{1,0:T(8,128)S(1)} %copy.21.bounds_ref, s32[1,7]{1,0:T(1,128)S(1)} %copy-done.12), custom_call_target="tpu_custom_call" | custom-call | flops 20000000000 | bytes 8000000 | tf_op jit(solution)/shard_map/attention/pallas_call | solution.py:550
  81.3 1.2 fusion.1
  82.5 0.0 copy-start.3
  82.5 0.0 all-to-all-done
  82.5 1.2 %copy_bitcast_fusion = bf16[2048,160]{0,1:T(8,128)(2,1)S(1)} fusion(bf16[128,16,160]{0,2,1:T(8,128)(2,1)} %all-to-all-done), kind=kLoop, calls=%fused_computation.6 | loop fusion | bytes 1310720 | tf_op jit(solution)/shard_map/all_to_all | solution.py:615
  83.7 5.1 %fusion.11 = (f32[128]{0:T(128)S(1)}, f32[128]{0:T(128)S(1)}, f32[128,1024]{1,0:T(8,128)S(1)}) fusion(f32[128]{0:T(128)S(1)} %add_rsqrt_fusion, f32[128,1024]{1,0:T(8,128)S(1)} %get-tuple-element.29, f32[128]{0:T(128)S(1)} %broadcast_multiply_fusion.2, f32[1024]{0:T(1024)S(1)} %copy-done.13, bf16[128,3072]{1,0:T(8,128)(2,1)S(1)} %get-tuple-element.21, ...), kind=kOutput, calls=%fused_computation.27 | convolution fusion | flops 806092544 | bytes 8132608 | tf_op jit(solution)/shard_map/dot_general | solution.py:20
  88.8 0.0 copy-done.3
  88.8 0.2 add_convert_fusion.x_ref
  89.0 0.0 copy-start.1
  89.0 27.2 %all_gather.1 = bf16[16,128,1024]{2,1,0:T(8,128)(2,1)S(1)} custom-call(bf16[128,1024]{1,0:T(8,128)(2,1)S(1)} %add_convert_fusion.x_ref), custom_call_target="tpu_custom_call" | custom-call | tf_op jit(solution)/shard_map/all_gather/pallas_call | solution.py:249
  116.2 1.7 %fusion.14 = f32[160,1024]{1,0:T(8,128)} fusion(bf16[2048,160]{0,1:T(8,128)(2,1)S(1)} %copy_bitcast_fusion, bf16[2048,1024]{1,0:T(8,128)(2,1)S(1)} %bitcast.20), kind=kOutput, calls=%fused_computation.30 | convolution fusion | flops 671088640 | bytes 5505024 | tf_op jit(solution)/shard_map/dot_general | solution.py:24
  117.9 0.0 copy-done.1
  (6 shorter events, 0.0 us)
Async XLA Ops:
  1.4 3.2 %collective-permute-start = (bf16[8,80]{0,1:T(8,128)(2,1)S(1)}, bf16[8,80]{0,1:T(8,128)(2,1)S(1)}, u32[]{:S(2)}, u32[]{:S(2)}) collective-permute-start(bf16[8,80]{0,1:T(8,128)(2,1)S(1)} %slice.27), channel_id=1, source_target_pairs={{0,1},{1,2},{2,3},{3,4},{4,5},{5,6},{6,7},{7,8},{8,9},{9,10},{10,1... | collective-permute-start | bytes 3848 | tf_op jit(solution)/shard_map/ppermute | solution.py:591
  7.1 1.0 copy-start.2
  8.0 0.9 copy-start.7
  8.9 0.9 copy-start.8
  9.8 0.7 copy-start.9
  10.5 0.7 copy-start.10
  11.2 0.7 copy-start.11
  29.9 3.9 %copy-start.13 = (f32[1024]{0:T(1024)S(1)}, f32[1024]{0:T(1024)}, u32[]{:S(2)}) copy-start(f32[1024]{0:T(1024)} %param.20) | copy-start | bytes 12292
  29.9 4.0 %copy-start = (bf16[1024,1024]{1,0:T(8,128)(2,1)S(1)}, bf16[1024,1024]{1,0:T(8,128)(2,1)}, u32[]{:S(2)}) copy-start(bf16[1024,1024]{1,0:T(8,128)(2,1)} %weight_ref.1) | copy-start | bytes 6291460
  49.6 1.3 %copy-start.4 = (bf16[896,1024]{1,0:T(8,128)(2,1)}, bf16[896,1024]{1,0:T(8,128)(2,1)S(1)}, u32[]{:S(2)}) copy-start(bf16[896,1024]{1,0:T(8,128)(2,1)S(1)} %get-tuple-element.17.do_ref) | copy-start | bytes 5505028
  50.8 1.2 %copy-start.6 = (bf16[7,128,1024]{2,1,0:T(8,128)(2,1)}, bf16[7,128,1024]{2,1,0:T(8,128)(2,1)S(1)}, u32[]{:S(2)}) copy-start(bf16[7,128,1024]{2,1,0:T(8,128)(2,1)S(1)} %get-tuple-element.15) | copy-start | bytes 5505028
  53.1 29.3 %all-to-all-start = ((bf16[128,16,160]{0,2,1:T(8,128)(2,1)}), bf16[128,16,160]{0,2,1:T(8,128)(2,1)}, u32[]{:S(2)}, u32[]{:S(2)}) async-start(bf16[128,16,160]{0,2,1:T(8,128)(2,1)} %bitcast.23), calls=%async_computation | async-start | bytes 1310720 | tf_op jit(solution)/shard_map/all_to_all | solution.py:615
  59.9 8.7 %copy-start.5 = (bf16[896,1024]{1,0:T(8,128)(2,1)S(1)}, bf16[896,1024]{1,0:T(8,128)(2,1)}, u32[]{:S(2)}) copy-start(bf16[896,1024]{1,0:T(8,128)(2,1)} %copy-done.4) | copy-start | bytes 5505028
  60.0 8.7 %copy-start.12 = (s32[1,7]{1,0:T(1,128)S(1)}, s32[1,7]{1,0:T(1,128)}, u32[]{:S(2)}) copy-start(s32[1,7]{1,0:T(1,128)} %live_ref.1) | copy-start | bytes 88
  82.5 6.3 %copy-start.3 = (bf16[128,1024]{1,0:T(8,128)(2,1)S(1)}, bf16[128,1024]{1,0:T(8,128)(2,1)}, u32[]{:S(2)}) copy-start(bf16[128,1024]{1,0:T(8,128)(2,1)} %cot_ref.1) | copy-start | bytes 786436
  89.0 28.9 %copy-start.1 = (bf16[128,1024]{1,0:T(8,128)(2,1)}, bf16[128,1024]{1,0:T(8,128)(2,1)S(1)}, u32[]{:S(2)}) copy-start(bf16[128,1024]{1,0:T(8,128)(2,1)S(1)} %add_convert_fusion.x_ref) | copy-start | bytes 786436
